TPU v7x, 32 devices: a whole 2x2x4 slice. The times are simulated.
32 devices in a mesh: dom: 16 (over z, y, x), feat: 2 (over core).
Axes of the slice: x: 2, y: 2, z: 4, core: 2. Of those that a mesh axis runs over, the one named last changes fastest.
Arguments:
- node_lat: bfloat16 [16384, 512], P('dom'), may hold values from -6 to 6
- edge_lat: bfloat16 [32768, 512], P(('dom', 'feat')), may hold values from -6 to 6
- edge_src: int32 [32768], P(('dom', 'feat')), may hold values from 0 to 1535
- edge_dst: int32 [32768], P(('dom', 'feat')), may hold values from 0 to 1023
- halo_rows: int32 [128, 64], P('dom'), may hold values from 0 to 1023
- probe_rows: int32 [256, 128], P(('dom', 'feat')), may hold values from 0 to 1023
- probe_slot: int32 [16384, 8], P(('dom', 'feat')), may hold values from 0 to 1023
- probe_wgt: float32 [16384, 8], P(('dom', 'feat')), may hold values from 0.05 to 0.3
- probe_embed: bfloat16 [16384, 512], P(('dom', 'feat')), may hold values from -6 to 6
- edge_first: bfloat16 [2, 1536, 512], replicated, may hold values from -0.15625 to 0.15625
- edge_second: bfloat16 [2, 512, 512], replicated, may hold values from -0.25 to 0.25
- node_first: bfloat16 [2, 1024, 512], replicated, may hold values from -0.1875 to 0.1875
- node_second: bfloat16 [2, 512, 512], replicated, may hold values from -0.25 to 0.25
- decode_first: bfloat16 [512, 512], replicated, may hold values from -0.25 to 0.25
- decode_second: bfloat16 [4, 512], replicated, may hold values from -0.25 to 0.25
Outputs:
- surface_out: bfloat16 [16384, 512], P('dom')
- fields: float32 [4, 16384], P(None, ('dom', 'feat'))
All inputs are finite; a program needn't handle non-finite values.
Results may differ from a plain program's by a relative error of at most 0.013.
Values may be sent and summed in bfloat16 or wider, within the bound.
No kernel may reach another device: no remote copies, remote signals or barrier semaphores. Data moves between devices by JAX's collectives and lax.ppermute only.
A program may use at most 64 MiB of HBM per device.

v0:
```python
import functools

import jax
import jax.numpy as jnp
from jax import lax
from jax.experimental import pallas as pl
from jax.experimental.pallas import tpu as pltpu
from jax.sharding import PartitionSpec as P

SPAN = 4
LANES = 128
CHUNK = 256
VMEM_GRANT = 24 << 20
BF16 = jnp.bfloat16
F32 = jnp.float32


def steps_of_pairs(width):
    return [1, width, width + 1, width - 1]


def both_ways(value, steps):
    count = lax.axis_size("dom")
    pairs = []
    for source in range(count):
        pairs.append((2 * source, 2 * ((source + steps) % count)))
        pairs.append((2 * source + 1, 2 * ((source - steps) % count) + 1))
    return lax.ppermute(value, ("dom", "feat"), pairs)


def swapped(value):
    return lax.ppermute(value, "feat", [(0, 1), (1, 0)])


def dot(left, right):
    return jnp.dot(left, right, preferred_element_type=F32)


def normed(values):
    shifted = values - jnp.mean(values, axis=-1, keepdims=True)
    spread = jnp.mean(shifted * shifted, axis=-1, keepdims=True)
    return shifted * lax.rsqrt(spread + 1e-05)


def columns_of(row):
    return jnp.broadcast_to(row, (LANES, row.shape[1])).T


def picks(columns, base, width):
    lane = lax.broadcasted_iota(jnp.int32, columns.shape, 1)
    parts = []
    for start in range(0, width, LANES):
        parts.append(jnp.where(columns == lane + (base + start), 1.0, 0.0).astype(BF16))
    return jnp.concatenate(parts, axis=1)


def index_columns(rows_ref, first, count):
    per = rows_ref.shape[1]
    rows = [columns_of(rows_ref[pl.ds(r, 1), :]) for r in range(first // per, (first + count) // per)]
    return jnp.concatenate(rows, axis=0) if len(rows) > 1 else rows[0]


def send_rows(side, lists_ref, first, table_ref, out_ref, at):
    row = jnp.where(side == 0, lists_ref[pl.ds(first, 1), :], lists_ref[pl.ds(first + 1, 1), :])
    select = picks(columns_of(row), 0, table_ref.shape[0])
    out_ref[at : at + row.shape[1], :] = dot(select, table_ref[...]).astype(BF16)


def halo_send_kernel(side_ref, rows_ref, nodes_ref, *out_refs):
    for i, out_ref in enumerate(out_refs):
        send_rows(side_ref[0], rows_ref, 2 * i, nodes_ref, out_ref, 0)


def edge_near_kernel(src_ref, dst_ref, nodes_ref, first_ref, near_ref, recv_ref, own_ref, *, layer):
    count, width = nodes_ref.shape
    own_ref[...] = dot(nodes_ref[...], first_ref[layer, width : 2 * width, :]).astype(BF16)
    recv_ref[...] = dot(nodes_ref[...], first_ref[layer, 2 * width : 3 * width, :]).astype(BF16)
    total_edges = near_ref.shape[0]
    for start in range(0, total_edges, CHUNK):
        total = dot(picks(index_columns(src_ref, start, CHUNK), 0, count), own_ref[...])
        if start < total_edges // 2:
            total += dot(picks(index_columns(dst_ref, start, CHUNK), 0, count), recv_ref[...])
        near_ref[start : start + CHUNK, :] = total


def halo_places(far, slot, side):
    block = far // slot
    place = (block // 2) * slot + far % slot
    kept = block % 2 == side
    inside = far >= 0
    mine = jnp.where(jnp.logical_and(inside, kept), place, -1)
    others = jnp.where(jnp.logical_and(inside, jnp.logical_not(kept)), place, -1)
    return mine, others


def edge_kept_kernel(
    side_ref, src_ref, dst_ref, edges_ref, recv_ref, kept_ref, first_ref, mid_ref, table_ref, *, layer, slot
):
    side = side_ref[0]
    half, width = kept_ref.shape
    count = recv_ref.shape[0]
    total_edges = edges_ref.shape[0]
    table_ref[...] = dot(kept_ref[...], first_ref[layer, width : 2 * width, :]).astype(BF16)
    for start in range(0, total_edges, CHUNK):
        span = slice(start, start + CHUNK)
        far = index_columns(src_ref, start, CHUNK) - count
        mine, _ = halo_places(far, slot, side)
        total = dot(edges_ref[span, :], first_ref[layer, 0:width, :])
        total += dot(picks(mine, 0, half), table_ref[...])
        if start >= total_edges // 2:
            total += dot(picks(index_columns(dst_ref, start, CHUNK), 0, count), recv_ref[...])
        mid_ref[span, :] = total


def edge_post_kernel(
    side_ref,
    src_ref,
    dst_ref,
    near_ref,
    mid_ref,
    edges_ref,
    other_ref,
    first_ref,
    second_ref,
    new_ref,
    part_ref,
    table_ref,
    *,
    layer,
    slot,
):
    side = side_ref[0]
    half, width = other_ref.shape
    count = part_ref.shape[0]
    total_edges = edges_ref.shape[0]
    table_ref[...] = dot(other_ref[...], first_ref[layer, width : 2 * width, :]).astype(BF16)
    for start in range(0, total_edges, CHUNK):
        span = slice(start, start + CHUNK)
        far = index_columns(src_ref, start, CHUNK) - count
        _, others = halo_places(far, slot, side)
        hidden = near_ref[span, :] + mid_ref[span, :] + dot(picks(others, 0, half), table_ref[...])
        hidden = jnp.maximum(hidden, 0.0).astype(BF16)
        update = normed(dot(hidden, second_ref[layer]))
        new_ref[span, :] = (edges_ref[span, :].astype(F32) + update).astype(BF16)
    for start in range(0, count, CHUNK):
        node = lax.broadcasted_iota(jnp.int32, (CHUNK, LANES), 0) + start
        parts = []
        for r in range(total_edges // LANES):
            row = jnp.broadcast_to(dst_ref[pl.ds(r, 1), :], (CHUNK, LANES))
            parts.append(jnp.where(row == node, 1.0, 0.0).astype(BF16))
        part_ref[start : start + CHUNK, :] = dot(
            jnp.concatenate(parts, axis=1), new_ref[...]
        ).astype(BF16)


def node_own_kernel(nodes_ref, first_ref, own_ref, *, layer):
    own_ref[...] = dot(nodes_ref[...], first_ref[layer, 0 : nodes_ref.shape[1], :])


def node_rows(layer, own_ref, part_ref, other_ref, nodes_ref, first_ref, second_ref, new_ref):
    count, width = nodes_ref.shape
    for start in range(0, count, CHUNK):
        span = slice(start, start + CHUNK)
        summed = (part_ref[span, :].astype(F32) + other_ref[span, :].astype(F32)).astype(BF16)
        hidden = own_ref[span, :] + dot(summed, first_ref[layer, width : 2 * width, :])
        hidden = jnp.maximum(hidden, 0.0).astype(BF16)
        update = normed(dot(hidden, second_ref[layer]))
        new_ref[span, :] = (nodes_ref[span, :].astype(F32) + update).astype(BF16)


def node_kernel(
    side_ref, rows_ref, own_ref, part_ref, other_ref, nodes_ref, first_ref, second_ref, new_ref, *out_refs, layer
):
    node_rows(layer, own_ref, part_ref, other_ref, nodes_ref, first_ref, second_ref, new_ref)
    for i, out_ref in enumerate(out_refs):
        send_rows(side_ref[0], rows_ref, 2 * i, new_ref, out_ref, 0)


def node_probe_kernel(
    side_ref,
    rows_ref,
    far_rows_ref,
    own_ref,
    part_ref,
    other_ref,
    nodes_ref,
    first_ref,
    second_ref,
    new_ref,
    *out_refs,
    layer,
):
    node_rows(layer, own_ref, part_ref, other_ref, nodes_ref, first_ref, second_ref, new_ref)
    slot = rows_ref.shape[1]
    for i, out_ref in enumerate(out_refs):
        send_rows(side_ref[0], rows_ref, 2 * i, new_ref, out_ref, 0)
        send_rows(side_ref[0], far_rows_ref, 2 * i, new_ref, out_ref, slot)


def weights_kernel(side_ref, slots_ref, wgt_ref, out_ref, *, slot):
    side = side_ref[0]
    half = out_ref.shape[1] // 2
    lane = lax.broadcasted_iota(jnp.int32, (LANES, LANES), 1)
    for start in range(0, out_ref.shape[0], LANES):
        places = []
        shares = []
        for k in range(slots_ref.shape[0]):
            pick = columns_of(slots_ref[pl.ds(k, 1), start : start + LANES])
            block = pick // slot
            place = (block // 2) * slot + pick % slot
            places.append(jnp.where(block % 2 == side, place, place + half))
            shares.append(columns_of(wgt_ref[pl.ds(k, 1), start : start + LANES]))
        for first in range(0, 2 * half, LANES):
            total = jnp.zeros((LANES, LANES), F32)
            for place, share in zip(places, shares):
                total += jnp.where(place == lane + first, share, 0.0)
            out_ref[start : start + LANES, first : first + LANES] = total.astype(BF16)


def decode_kernel(table_ref, embed_ref, first_ref, second_ref, a_ref, b_ref, c_ref, d_ref, other_ref, out_ref):
    slot = a_ref.shape[0] // 2
    half = 4 * slot
    interp = dot(table_ref[:, half:], other_ref[...])
    for i, ref in enumerate((a_ref, b_ref, c_ref, d_ref)):
        interp += dot(table_ref[:, i * slot : (i + 1) * slot], ref[0:slot, :])
    decoder_in = (interp + embed_ref[...].astype(F32)).astype(BF16)
    hidden = jnp.maximum(dot(decoder_in, first_ref[...]), 0.0).astype(BF16)
    out_ref[...] = lax.dot_general(
        second_ref[...], hidden, (((1,), (1,)), ((), ())), preferred_element_type=F32
    )


SCALAR = pl.BlockSpec(memory_space=pltpu.SMEM)
ON_CHIP = pl.BlockSpec(memory_space=pltpu.VMEM)


def run(kernel, flops, outs, args, scratch=()):
    nbytes = sum(a.size * a.dtype.itemsize for a in args)
    return pl.pallas_call(
        kernel,
        in_specs=[SCALAR if a.ndim == 1 else ON_CHIP for a in args],
        out_specs=[ON_CHIP] * len(outs),
        out_shape=[jax.ShapeDtypeStruct(shape, dtype) for shape, dtype in outs],
        scratch_shapes=list(scratch),
        compiler_params=pltpu.CompilerParams(vmem_limit_bytes=VMEM_GRANT),
        cost_estimate=pl.CostEstimate(flops=flops, bytes_accessed=nbytes, transcendentals=0),
    )(*args)


def exchanged(pieces, steps):
    got = []
    for piece, step in zip(pieces, steps):
        got.append(both_ways(piece, step))
    return got


def one_layer(layer, last, side, h, e, sends, src, dst, halo_rows, probe_rows, far_rows, weights):
    edge_first, edge_second, node_first, node_second = weights
    steps = steps_of_pairs(SPAN)
    pairs = len(steps)
    nodes, width = h.shape
    edges = e.shape[0]
    slot = halo_rows.shape[1]
    half = pairs * slot
    kept = jnp.concatenate(exchanged(sends, steps), axis=0)
    near, recv = run(
        functools.partial(edge_near_kernel, layer=layer),
        4 * nodes * width * width + 3 * edges * nodes * width,
        [((edges, width), F32), ((nodes, width), BF16)],
        (src, dst, h, edge_first),
        [pltpu.VMEM((nodes, width), BF16)],
    )
    other = swapped(kept)
    (mid,) = run(
        functools.partial(edge_kept_kernel, layer=layer, slot=slot),
        2 * width * (half * (width + edges) + edges * width) + edges * nodes * width,
        [((edges, width), F32)],
        (side, src, dst, e, recv, kept, edge_first),
        [pltpu.VMEM((half, width), BF16)],
    )
    e, part = run(
        functools.partial(edge_post_kernel, layer=layer, slot=slot),
        2 * width * (half * (width + edges) + edges * (width + nodes)),
        [((edges, width), BF16), ((nodes, width), BF16)],
        (side, src, dst, near, mid, e, other, edge_first, edge_second),
        [pltpu.VMEM((half, width), BF16)],
    )
    part_other = swapped(part)
    (own,) = run(
        functools.partial(node_own_kernel, layer=layer),
        2 * nodes * width * width,
        [((nodes, width), F32)],
        (h, node_first),
    )
    node_args = (own, part, part_other, h, node_first, node_second)
    node_flops = 4 * nodes * width * width
    if not last:
        h, *sends = run(
            functools.partial(node_kernel, layer=layer),
            node_flops + 2 * half * nodes * width,
            [((nodes, width), BF16)] + [((slot, width), BF16)] * pairs,
            (side, halo_rows) + node_args,
        )
    else:
        qslot = probe_rows.shape[1]
        h, *sends = run(
            functools.partial(node_probe_kernel, layer=layer),
            node_flops + 4 * pairs * qslot * nodes * width,
            [((nodes, width), BF16)] + [((2 * qslot, width), BF16)] * pairs,
            (side, probe_rows, far_rows) + node_args,
        )
    return h, e, sends


def body(
    node_lat,
    edge_lat,
    edge_src,
    edge_dst,
    halo_rows,
    probe_rows,
    probe_slot,
    probe_wgt,
    probe_embed,
    edge_first,
    edge_second,
    node_first,
    node_second,
    decode_first,
    decode_second,
):
    steps = steps_of_pairs(SPAN)
    pairs = len(steps)
    side = lax.axis_index("feat").astype(jnp.int32).reshape(1)
    nodes, width = node_lat.shape
    edges = edge_lat.shape[0]
    slot = halo_rows.shape[1]
    qslot = probe_rows.shape[1]
    probes = probe_slot.shape[0]
    layers = edge_first.shape[0]
    src = edge_src.reshape(edges // LANES, LANES)
    dst = edge_dst.reshape(edges // LANES, LANES)
    weights = (edge_first, edge_second, node_first, node_second)
    h = node_lat
    e = edge_lat
    sends = run(
        halo_send_kernel,
        2 * pairs * slot * nodes * width,
        [((slot, width), BF16)] * pairs,
        (side, halo_rows, h),
    )
    far_rows = swapped(probe_rows)
    for layer in range(layers):
        h, e, sends = one_layer(
            layer, layer + 1 == layers, side, h, e, sends, src, dst, halo_rows, probe_rows, far_rows, weights
        )
    got = exchanged(sends, steps)
    slots_t = probe_slot.T
    wgt_t = probe_wgt.T
    (table,) = run(
        functools.partial(weights_kernel, slot=qslot),
        8 * probes * pairs * 2 * qslot * pairs * 2,
        [((probes, 2 * pairs * qslot), BF16)],
        (side, slots_t, wgt_t),
    )
    other = swapped(jnp.concatenate([piece[qslot:] for piece in got], axis=0))
    (fields,) = run(
        decode_kernel,
        2 * probes * width * (2 * pairs * qslot + width),
        [((decode_second.shape[0], probes), F32)],
        (table, probe_embed, decode_first, decode_second, *got, other),
    )
    return (h, fields)


def solution(mesh):
    return jax.shard_map(
        body,
        mesh=mesh,
        in_specs=(
            P("dom", None),
            P(("dom", "feat"), None),
            P(("dom", "feat")),
            P(("dom", "feat")),
            P("dom", None),
            P(("dom", "feat"), None),
            P(("dom", "feat"), None),
            P(("dom", "feat"), None),
            P(("dom", "feat"), None),
            P(),
            P(),
            P(),
            P(),
            P(),
            P(),
        ),
        out_specs=(P("dom", None), P(None, ("dom", "feat"))),
        check_vma=False,
    )
```

profile of v0, /device:TPU:0, one launch (start us, length us, event | category | flops | bytes accessed | tf_op | source)
XLA Modules:
  0.0 95.6 jit_solution(14785104160000980636)
XLA Ops:
  0.6 1.2 %copy-done.3 = bf16[1024,512]{1,0:T(8,128)(2,1)S(1)} copy-done((bf16[1024,512]{1,0:T(8,128)(2,1)S(1)}, bf16[1024,512]{1,0:T(8,128)(2,1)}, u32[]{:S(2)}) %copy-start.3) | copy-done | bytes 1048600
  1.9 0.7 copy-done.16
  2.5 0.9 shard_map.160
  3.4 3.0 %collective-permute-start.1 = (bf16[64,512]{1,0:T(8,128)(2,1)S(1)}, bf16[64,512]{1,0:T(8,128)(2,1)S(1)}, u32[]{:S(2)}, u32[]{:S(2)}) collective-permute-start(bf16[64,512]{1,0:T(8,128)(2,1)S(1)} %get-tuple-element.25), channel_id=1, source_target_pairs={{0,2},{1,31},{2,4},{3,1},{4,6},{5,3},{6,8},{7,5},{8,10},{9,7},{10,... | collective-permute-start | bytes 196616 | tf_op jit(solution)/shard_map/ppermute | solution.py:28
  6.5 1.6 %collective-permute-start.2 = (bf16[64,512]{1,0:T(8,128)(2,1)S(1)}, bf16[64,512]{1,0:T(8,128)(2,1)S(1)}, u32[]{:S(2)}, u32[]{:S(2)}) collective-permute-start(bf16[64,512]{1,0:T(8,128)(2,1)S(1)} %get-tuple-element.26), channel_id=1, source_target_pairs={{0,8},{1,25},{2,10},{3,27},{4,12},{5,29},{6,14},{7,31},{8,16},{9,1... | collective-permute-start | bytes 196616 | tf_op jit(solution)/shard_map/ppermute | solution.py:28
  8.0 2.5 %collective-permute-start.3 = (bf16[64,512]{1,0:T(8,128)(2,1)S(1)}, bf16[64,512]{1,0:T(8,128)(2,1)S(1)}, u32[]{:S(2)}, u32[]{:S(2)}) collective-permute-start(bf16[64,512]{1,0:T(8,128)(2,1)S(1)} %get-tuple-element.27), channel_id=1, source_target_pairs={{0,10},{1,23},{2,12},{3,25},{4,14},{5,27},{6,16},{7,29},{8,18},{9,... | collective-permute-start | bytes 196616 | tf_op jit(solution)/shard_map/ppermute | solution.py:28
  10.5 2.4 %collective-permute-start.4 = (bf16[64,512]{1,0:T(8,128)(2,1)S(1)}, bf16[64,512]{1,0:T(8,128)(2,1)S(1)}, u32[]{:S(2)}, u32[]{:S(2)}) collective-permute-start(bf16[64,512]{1,0:T(8,128)(2,1)S(1)} %get-tuple-element.28), channel_id=1, source_target_pairs={{0,6},{1,27},{2,8},{3,29},{4,10},{5,31},{6,12},{7,1},{8,14},{9,3},... | collective-permute-start | bytes 196616 | tf_op jit(solution)/shard_map/ppermute | solution.py:28
  13.0 0.3 collective-permute-done.1
  13.4 1.9 %collective-permute-done.3 = bf16[64,512]{1,0:T(8,128)(2,1)S(1)} collective-permute-done((bf16[64,512]{1,0:T(8,128)(2,1)S(1)}, bf16[64,512]{1,0:T(8,128)(2,1)S(1)}, u32[]{:S(2)}, u32[]{:S(2)}) %collective-permute-start.3) | collective-permute-done | bytes 65568 | tf_op jit(solution)/shard_map/ppermute | solution.py:28
  15.2 2.3 %collective-permute-done.4 = bf16[64,512]{1,0:T(8,128)(2,1)S(1)} collective-permute-done((bf16[64,512]{1,0:T(8,128)(2,1)S(1)}, bf16[64,512]{1,0:T(8,128)(2,1)S(1)}, u32[]{:S(2)}, u32[]{:S(2)}) %collective-permute-start.4) | collective-permute-done | bytes 65568 | tf_op jit(solution)/shard_map/ppermute | solution.py:28
  17.5 1.9 %copy-done = bf16[2,1536,512]{2,1,0:T(8,128)(2,1)S(1)} copy-done((bf16[2,1536,512]{2,1,0:T(8,128)(2,1)S(1)}, bf16[2,1536,512]{2,1,0:T(8,128)(2,1)}, u32[]{:S(2)}) %copy-start) | copy-done | bytes 3145752
  19.4 0.7 copy-done.10
  20.1 0.7 copy-done.12
  20.8 3.1 %shard_map.159 = (f32[1024,512]{1,0:T(8,128)S(1)}, bf16[1024,512]{1,0:T(8,128)(2,1)S(1)}) custom-call(s32[8,128]{1,0:T(8,128)S(1)} %bitcast.5, s32[8,128]{1,0:T(8,128)S(1)} %bitcast.11, bf16[1024,512]{1,0:T(8,128)(2,1)S(1)} %copy-done.3, bf16[2,1536,512]{2,1,0:T(8,128)(2,1)S(1)} %copy-done), custom_call_target="tpu_custom_call" | custom-call | flops 2684354560 | bytes 4202496 | tf_op jit(solution)/shard_map/pallas_call | solution.py:239
  23.9 0.0 copy-start.7
  24.0 0.0 copy-start.11
  24.0 2.3 %shard_map.161.mid_ref = f32[1024,512]{1,0:T(8,128)S(1)} custom-call(s32[1]{0:T(128)} %bitcast.side_ref, s32[8,128]{1,0:T(8,128)S(1)} %bitcast.6, s32[8,128]{1,0:T(8,128)S(1)} %bitcast.12, bf16[1024,512]{1,0:T(8,128)(2,1)S(1)} %copy-done.5, bf16[1024,512]{1,0:T(8,128)(2,1)S(1)} %get-tuple-element.24.recv_ref, ...), custom_call_target="tpu_custom_call" | custom-call | flops 1476395008 | bytes 5513220 | tf_op jit(solution)/shard_map/pallas_call | solution.py:239
  26.3 3.6 %shard_map.162 = (bf16[1024,512]{1,0:T(8,128)(2,1)S(1)}, bf16[1024,512]{1,0:T(8,128)(2,1)S(1)}) custom-call(s32[1]{0:T(128)} %bitcast.side_ref, s32[8,128]{1,0:T(8,128)S(1)} %bitcast.7, s32[8,128]{1,0:T(8,128)S(1)} %bitcast.13, f32[1024,512]{1,0:T(8,128)S(1)} %get-tuple-element.23.near_ref, f32[1024,512]{1,0:T(8,128)S(1)} %shard_map.161.mid_ref, ...), custom_call_target="tpu_custom_call" | custom-call | flops 2013265920 | bytes 9707524 | tf_op jit(solution)/shard_map/pallas_call | solution.py:239
  29.9 0.0 copy-start.6
  29.9 0.0 copy-start.17
  30.0 0.6 collective-permute-start.6
  30.5 0.7 shard_map.158.own_ref
  31.2 1.6 %collective-permute-done.6.other_ref = bf16[1024,512]{1,0:T(8,128)(2,1)S(1)} collective-permute-done((bf16[1024,512]{1,0:T(8,128)(2,1)S(1)}, bf16[1024,512]{1,0:T(8,128)(2,1)S(1)}, u32[]{:S(2)}, u32[]{:S(2)}) %collective-permute-start.6) | collective-permute-done | bytes 1048608 | tf_op jit(solution)/shard_map/ppermute | solution.py:32
  32.8 2.7 %shard_map.163 = (bf16[1024,512]{1,0:T(8,128)(2,1)S(1)}, bf16[64,512]{1,0:T(8,128)(2,1)S(1)}, bf16[64,512]{1,0:T(8,128)(2,1)S(1)}, bf16[64,512]{1,0:T(8,128)(2,1)S(1)}, bf16[64,512]{1,0:T(8,128)(2,1)S(1)}) custom-call(s32[1]{0:T(128)} %bitcast.side_ref, s32[8,64]{1,0:T(8,128)S(1)} %copy-done.17, f32[1024,512]{1,0:T(8,128)S(1)} %shard_map.158.own_ref, ...), custom_call_target="tpu_custom_call" | custom-call | flops 1342177280 | bytes 8390660 | tf_op jit(solution)/shard_map/pallas_call | solution.py:239
  35.5 2.4 %collective-permute-start.7 = (bf16[64,512]{1,0:T(8,128)(2,1)S(1)}, bf16[64,512]{1,0:T(8,128)(2,1)S(1)}, u32[]{:S(2)}, u32[]{:S(2)}) collective-permute-start(bf16[64,512]{1,0:T(8,128)(2,1)S(1)} %get-tuple-element.34), channel_id=1, source_target_pairs={{0,2},{1,31},{2,4},{3,1},{4,6},{5,3},{6,8},{7,5},{8,10},{9,7},{10,... | collective-permute-start | bytes 196616 | tf_op jit(solution)/shard_map/ppermute | solution.py:28
  37.9 0.5 collective-permute-start.9
  38.5 2.8 %collective-permute-start.10 = (bf16[64,512]{1,0:T(8,128)(2,1)S(1)}, bf16[64,512]{1,0:T(8,128)(2,1)S(1)}, u32[]{:S(2)}, u32[]{:S(2)}) collective-permute-start(bf16[64,512]{1,0:T(8,128)(2,1)S(1)} %get-tuple-element.37), channel_id=1, source_target_pairs={{0,6},{1,27},{2,8},{3,29},{4,10},{5,31},{6,12},{7,1},{8,14},{9,3},... | collective-permute-start | bytes 196616 | tf_op jit(solution)/shard_map/ppermute | solution.py:28
  41.3 2.8 %collective-permute-done.7 = bf16[64,512]{1,0:T(8,128)(2,1)S(1)} collective-permute-done((bf16[64,512]{1,0:T(8,128)(2,1)S(1)}, bf16[64,512]{1,0:T(8,128)(2,1)S(1)}, u32[]{:S(2)}, u32[]{:S(2)}) %collective-permute-start.7) | collective-permute-done | bytes 65568 | tf_op jit(solution)/shard_map/ppermute | solution.py:28
  44.1 0.2 collective-permute-done.8
  44.3 3.1 %collective-permute-done.9 = bf16[64,512]{1,0:T(8,128)(2,1)S(1)} collective-permute-done((bf16[64,512]{1,0:T(8,128)(2,1)S(1)}, bf16[64,512]{1,0:T(8,128)(2,1)S(1)}, u32[]{:S(2)}, u32[]{:S(2)}) %collective-permute-start.9) | collective-permute-done | bytes 65568 | tf_op jit(solution)/shard_map/ppermute | solution.py:28
  47.3 0.1 collective-permute-start.11
  47.4 3.1 %shard_map.165 = (f32[1024,512]{1,0:T(8,128)S(1)}, bf16[1024,512]{1,0:T(8,128)(2,1)S(1)}) custom-call(s32[8,128]{1,0:T(8,128)S(1)} %bitcast.8, s32[8,128]{1,0:T(8,128)S(1)} %bitcast.14, bf16[1024,512]{1,0:T(8,128)(2,1)S(1)} %get-tuple-element.30.nodes_ref, bf16[2,1536,512]{2,1,0:T(8,128)(2,1)S(1)} %copy-done.1), custom_call_target="tpu_custom_call" | custom-call | flops 2684354560 | bytes 4202496 | tf_op jit(solution)/shard_map/pallas_call | solution.py:239
  50.5 2.3 %shard_map.166.mid_ref = f32[1024,512]{1,0:T(8,128)S(1)} custom-call(s32[1]{0:T(128)} %bitcast.side_ref, s32[8,128]{1,0:T(8,128)S(1)} %bitcast.9, s32[8,128]{1,0:T(8,128)S(1)} %bitcast.15, bf16[1024,512]{1,0:T(8,128)(2,1)S(1)} %get-tuple-element.32.edges_ref, bf16[1024,512]{1,0:T(8,128)(2,1)S(1)} %get-tuple-element.33.recv_ref, ...), custom_call_target="tpu_custom_call" | custom-call | flops 1476395008 | bytes 5513220 | tf_op jit(solution)/shard_map/pallas_call | solution.py:239
  52.9 4.3 %shard_map.167 = (bf16[1024,512]{1,0:T(8,128)(2,1)}, bf16[1024,512]{1,0:T(8,128)(2,1)S(1)}) custom-call(s32[1]{0:T(128)} %bitcast.side_ref, s32[8,128]{1,0:T(8,128)S(1)} %bitcast.10, s32[8,128]{1,0:T(8,128)S(1)} %bitcast.16, f32[1024,512]{1,0:T(8,128)S(1)} %get-tuple-element.31.near_ref, f32[1024,512]{1,0:T(8,128)S(1)} %shard_map.166.mid_ref, ...), custom_call_target="tpu_custom_call" | custom-call | flops 2013265920 | bytes 9707524 | tf_op jit(solution)/shard_map/pallas_call | solution.py:239
  57.2 0.5 collective-permute-start.12
  57.7 0.0 collective-permute-start
  57.7 0.7 shard_map.164.own_ref
  58.4 1.6 %collective-permute-done.far_rows_ref = s32[8,128]{1,0:T(8,128)S(1)} collective-permute-done((s32[8,128]{1,0:T(8,128)S(1)}, s32[8,128]{1,0:T(8,128)S(1)}, u32[]{:S(2)}, u32[]{:S(2)}) %collective-permute-start) | collective-permute-done | bytes 4128 | tf_op jit(solution)/shard_map/ppermute | solution.py:32
  60.0 3.6 %shard_map.168 = (bf16[1024,512]{1,0:T(8,128)(2,1)}, bf16[256,512]{1,0:T(8,128)(2,1)S(1)}, bf16[256,512]{1,0:T(8,128)(2,1)S(1)}, bf16[256,512]{1,0:T(8,128)(2,1)S(1)}, bf16[256,512]{1,0:T(8,128)(2,1)S(1)}) custom-call(s32[1]{0:T(128)} %bitcast.side_ref, s32[8,128]{1,0:T(8,128)S(1)} %copy-done.18, s32[8,128]{1,0:T(8,128)S(1)} %collective-permute-done.far_rows_ref, ...), custom_call_target="tpu_custom_call" | custom-call | flops 2147483648 | bytes 8396804 | tf_op jit(solution)/shard_map/pallas_call | solution.py:239
  63.6 0.0 copy-start.19
  63.6 1.1 %collective-permute-start.13 = (bf16[256,512]{1,0:T(8,128)(2,1)S(1)}, bf16[256,512]{1,0:T(8,128)(2,1)S(1)}, u32[]{:S(2)}, u32[]{:S(2)}) collective-permute-start(bf16[256,512]{1,0:T(8,128)(2,1)S(1)} %get-tuple-element.40), channel_id=1, source_target_pairs={{0,2},{1,31},{2,4},{3,1},{4,6},{5,3},{6,8},{7,5},{8,10},{9,7},{10,... | collective-permute-start | bytes 786440 | tf_op jit(solution)/shard_map/ppermute | solution.py:28
  64.7 2.1 %collective-permute-start.15 = (bf16[256,512]{1,0:T(8,128)(2,1)S(1)}, bf16[256,512]{1,0:T(8,128)(2,1)S(1)}, u32[]{:S(2)}, u32[]{:S(2)}) collective-permute-start(bf16[256,512]{1,0:T(8,128)(2,1)S(1)} %get-tuple-element.42), channel_id=1, source_target_pairs={{0,10},{1,23},{2,12},{3,25},{4,14},{5,27},{6,16},{7,29},{8,18},{9,... | collective-permute-start | bytes 786440 | tf_op jit(solution)/shard_map/ppermute | solution.py:28
  66.8 1.5 %collective-permute-start.16 = (bf16[256,512]{1,0:T(8,128)(2,1)S(1)}, bf16[256,512]{1,0:T(8,128)(2,1)S(1)}, u32[]{:S(2)}, u32[]{:S(2)}) collective-permute-start(bf16[256,512]{1,0:T(8,128)(2,1)S(1)} %get-tuple-element.43), channel_id=1, source_target_pairs={{0,6},{1,27},{2,8},{3,29},{4,10},{5,31},{6,12},{7,1},{8,14},{9,3},... | collective-permute-start | bytes 786440 | tf_op jit(solution)/shard_map/ppermute | solution.py:28
  68.3 8.2 %collective-permute-done.13.a_ref = bf16[256,512]{1,0:T(8,128)(2,1)S(1)} collective-permute-done((bf16[256,512]{1,0:T(8,128)(2,1)S(1)}, bf16[256,512]{1,0:T(8,128)(2,1)S(1)}, u32[]{:S(2)}, u32[]{:S(2)}) %collective-permute-start.13) | collective-permute-done | bytes 262176 | tf_op jit(solution)/shard_map/ppermute | solution.py:28
  76.5 11.1 %collective-permute-done.15.c_ref = bf16[256,512]{1,0:T(8,128)(2,1)S(1)} collective-permute-done((bf16[256,512]{1,0:T(8,128)(2,1)S(1)}, bf16[256,512]{1,0:T(8,128)(2,1)S(1)}, u32[]{:S(2)}, u32[]{:S(2)}) %collective-permute-start.15) | collective-permute-done | bytes 262176 | tf_op jit(solution)/shard_map/ppermute | solution.py:28
  87.8 0.1 collective-permute-start.17
  87.9 5.6 %shard_map.169.table_ref = bf16[512,1024]{1,0:T(8,128)(2,1)S(1)} custom-call(s32[1]{0:T(128)} %bitcast.side_ref, s32[8,512]{1,0:T(8,128)S(1)} %bitcast.17, f32[8,512]{1,0:T(8,128)S(1)} %bitcast.18), custom_call_target="tpu_custom_call" | custom-call | flops 33554432 | bytes 32772 | tf_op jit(solution)/shard_map/pallas_call | solution.py:239
  93.5 2.0 %shard_map.170 = f32[4,512]{1,0:T(4,128)} custom-call(bf16[512,1024]{1,0:T(8,128)(2,1)S(1)} %shard_map.169.table_ref, bf16[512,512]{1,0:T(8,128)(2,1)S(1)} %copy-done.8, bf16[512,512]{1,0:T(8,128)(2,1)S(1)} %copy-done.9, bf16[4,512]{1,0:T(4,128)(2,1)S(1)} %copy-done.19, bf16[256,512]{1,0:T(8,128)(2,1)S(1)} %collective-permute-done.13.a_ref, ...), custom_call_target="tpu_custom_call" | custom-call | flops 805306368 | bytes 3674112 | tf_op jit(solution)/shard_map/pallas_call | solution.py:239
  (54 shorter events, 0.2 us)
Async XLA Ops:
  0.6 1.2 %copy-start.3 = (bf16[1024,512]{1,0:T(8,128)(2,1)S(1)}, bf16[1024,512]{1,0:T(8,128)(2,1)}, u32[]{:S(2)}) copy-start(bf16[1024,512]{1,0:T(8,128)(2,1)} %nodes_ref.7) | copy-start | bytes 3145732
  1.9 0.7 copy-start.16
  3.4 9.9 %collective-permute-start.1 = (bf16[64,512]{1,0:T(8,128)(2,1)S(1)}, bf16[64,512]{1,0:T(8,128)(2,1)S(1)}, u32[]{:S(2)}, u32[]{:S(2)}) collective-permute-start(bf16[64,512]{1,0:T(8,128)(2,1)S(1)} %get-tuple-element.25), channel_id=1, source_target_pairs={{0,2},{1,31},{2,4},{3,1},{4,6},{5,3},{6,8},{7,5},{8,10},{9,7},{10,... | collective-permute-start | bytes 196616 | tf_op jit(solution)/shard_map/ppermute | solution.py:28
  6.5 6.9 %collective-permute-start.2 = (bf16[64,512]{1,0:T(8,128)(2,1)S(1)}, bf16[64,512]{1,0:T(8,128)(2,1)S(1)}, u32[]{:S(2)}, u32[]{:S(2)}) collective-permute-start(bf16[64,512]{1,0:T(8,128)(2,1)S(1)} %get-tuple-element.26), channel_id=1, source_target_pairs={{0,8},{1,25},{2,10},{3,27},{4,12},{5,29},{6,14},{7,31},{8,16},{9,1... | collective-permute-start | bytes 196616 | tf_op jit(solution)/shard_map/ppermute | solution.py:28
  8.0 7.2 %collective-permute-start.3 = (bf16[64,512]{1,0:T(8,128)(2,1)S(1)}, bf16[64,512]{1,0:T(8,128)(2,1)S(1)}, u32[]{:S(2)}, u32[]{:S(2)}) collective-permute-start(bf16[64,512]{1,0:T(8,128)(2,1)S(1)} %get-tuple-element.27), channel_id=1, source_target_pairs={{0,10},{1,23},{2,12},{3,25},{4,14},{5,27},{6,16},{7,29},{8,18},{9,... | collective-permute-start | bytes 196616 | tf_op jit(solution)/shard_map/ppermute | solution.py:28
  10.5 7.0 %collective-permute-start.4 = (bf16[64,512]{1,0:T(8,128)(2,1)S(1)}, bf16[64,512]{1,0:T(8,128)(2,1)S(1)}, u32[]{:S(2)}, u32[]{:S(2)}) collective-permute-start(bf16[64,512]{1,0:T(8,128)(2,1)S(1)} %get-tuple-element.28), channel_id=1, source_target_pairs={{0,6},{1,27},{2,8},{3,29},{4,10},{5,31},{6,12},{7,1},{8,14},{9,3},... | collective-permute-start | bytes 196616 | tf_op jit(solution)/shard_map/ppermute | solution.py:28
  17.5 8.8 %collective-permute-start.5 = (bf16[256,512]{1,0:T(8,128)(2,1)S(1)}, bf16[256,512]{1,0:T(8,128)(2,1)S(1)}, u32[]{:S(2)}, u32[]{:S(2)}) collective-permute-start(bf16[256,512]{1,0:T(8,128)(2,1)S(1)} %constant_dynamic-update-slice_fusion.kept_ref), channel_id=1, source_target_pairs={{0,1},{1,0},{2,3},{3,2},{4,5},{5,4},{6,7},{7,6},{8,9},{9,8},{10,11... | collective-permute-start | bytes 786440 | tf_op jit(solution)/shard_map/ppermute | solution.py:32
  17.5 1.9 %copy-start = (bf16[2,1536,512]{2,1,0:T(8,128)(2,1)S(1)}, bf16[2,1536,512]{2,1,0:T(8,128)(2,1)}, u32[]{:S(2)}) copy-start(bf16[2,1536,512]{2,1,0:T(8,128)(2,1)} %first_ref.19) | copy-start | bytes 9437188
  19.4 0.7 copy-start.10
  20.1 0.7 copy-start.12
  20.8 3.1 %copy-start.1 = (bf16[2,1536,512]{2,1,0:T(8,128)(2,1)S(1)}, bf16[2,1536,512]{2,1,0:T(8,128)(2,1)}, u32[]{:S(2)}) copy-start(bf16[2,1536,512]{2,1,0:T(8,128)(2,1)} %first_ref.19) | copy-start | bytes 9437188
  20.8 3.1 %copy-start.5 = (bf16[1024,512]{1,0:T(8,128)(2,1)S(1)}, bf16[1024,512]{1,0:T(8,128)(2,1)}, u32[]{:S(2)}) copy-start(bf16[1024,512]{1,0:T(8,128)(2,1)} %edges_ref.3) | copy-start | bytes 3145732
  23.9 2.3 %copy-start.7 = (bf16[2,512,512]{2,1,0:T(8,128)(2,1)S(1)}, bf16[2,512,512]{2,1,0:T(8,128)(2,1)}, u32[]{:S(2)}) copy-start(bf16[2,512,512]{2,1,0:T(8,128)(2,1)} %second_ref.7) | copy-start | bytes 3145732
  24.0 2.3 %copy-start.11 = (s32[1024]{0:T(1024)S(1)}, s32[1024]{0:T(1024)}, u32[]{:S(2)}) copy-start(s32[1024]{0:T(1024)} %param.17) | copy-start | bytes 12292
  24.0 2.3 %copy-start.13 = (s32[1024]{0:T(1024)S(1)}, s32[1024]{0:T(1024)}, u32[]{:S(2)}) copy-start(s32[1024]{0:T(1024)} %param.18) | copy-start | bytes 12292
  26.3 4.2 %copy-start.2 = (bf16[2,1024,512]{2,1,0:T(8,128)(2,1)S(1)}, bf16[2,1024,512]{2,1,0:T(8,128)(2,1)}, u32[]{:S(2)}) copy-start(bf16[2,1024,512]{2,1,0:T(8,128)(2,1)} %first_ref.20) | copy-start | bytes 6291460
  26.3 4.2 %copy-start.4 = (bf16[1024,512]{1,0:T(8,128)(2,1)S(1)}, bf16[1024,512]{1,0:T(8,128)(2,1)}, u32[]{:S(2)}) copy-start(bf16[1024,512]{1,0:T(8,128)(2,1)} %nodes_ref.7) | copy-start | bytes 3145732
  29.9 2.9 %copy-start.6 = (bf16[2,512,512]{2,1,0:T(8,128)(2,1)S(1)}, bf16[2,512,512]{2,1,0:T(8,128)(2,1)}, u32[]{:S(2)}) copy-start(bf16[2,512,512]{2,1,0:T(8,128)(2,1)} %second_ref.8) | copy-start | bytes 3145732
  29.9 2.9 %copy-start.17 = (s32[8,64]{1,0:T(8,128)S(1)}, s32[8,64]{1,0:T(8,128)}, u32[]{:S(2)}) copy-start(s32[8,64]{1,0:T(8,128)} %rows_ref.4) | copy-start | bytes 6148
  30.0 2.8 %collective-permute-start.6 = (bf16[1024,512]{1,0:T(8,128)(2,1)S(1)}, bf16[1024,512]{1,0:T(8,128)(2,1)S(1)}, u32[]{:S(2)}, u32[]{:S(2)}) collective-permute-start(bf16[1024,512]{1,0:T(8,128)(2,1)S(1)} %get-tuple-element.29.part_ref), channel_id=1, source_target_pairs={{0,1},{1,0},{2,3},{3,2},{4,5},{5,4},{6,7},{7,6},{8,9},{9,8},{10,11... | collective-permute-start | bytes 3145736 | tf_op jit(solution)/shard_map/ppermute | solution.py:32
  35.5 8.6 %collective-permute-start.7 = (bf16[64,512]{1,0:T(8,128)(2,1)S(1)}, bf16[64,512]{1,0:T(8,128)(2,1)S(1)}, u32[]{:S(2)}, u32[]{:S(2)}) collective-permute-start(bf16[64,512]{1,0:T(8,128)(2,1)S(1)} %get-tuple-element.34), channel_id=1, source_target_pairs={{0,2},{1,31},{2,4},{3,1},{4,6},{5,3},{6,8},{7,5},{8,10},{9,7},{10,... | collective-permute-start | bytes 196616 | tf_op jit(solution)/shard_map/ppermute | solution.py:28
  37.9 6.3 %collective-permute-start.8 = (bf16[64,512]{1,0:T(8,128)(2,1)S(1)}, bf16[64,512]{1,0:T(8,128)(2,1)S(1)}, u32[]{:S(2)}, u32[]{:S(2)}) collective-permute-start(bf16[64,512]{1,0:T(8,128)(2,1)S(1)} %get-tuple-element.35), channel_id=1, source_target_pairs={{0,8},{1,25},{2,10},{3,27},{4,12},{5,29},{6,14},{7,31},{8,16},{9,1... | collective-permute-start | bytes 196616 | tf_op jit(solution)/shard_map/ppermute | solution.py:28
  37.9 9.4 %collective-permute-start.9 = (bf16[64,512]{1,0:T(8,128)(2,1)S(1)}, bf16[64,512]{1,0:T(8,128)(2,1)S(1)}, u32[]{:S(2)}, u32[]{:S(2)}) collective-permute-start(bf16[64,512]{1,0:T(8,128)(2,1)S(1)} %get-tuple-element.36), channel_id=1, source_target_pairs={{0,10},{1,23},{2,12},{3,25},{4,14},{5,27},{6,16},{7,29},{8,18},{9,... | collective-permute-start | bytes 196616 | tf_op jit(solution)/shard_map/ppermute | solution.py:28
  38.5 8.8 %collective-permute-start.10 = (bf16[64,512]{1,0:T(8,128)(2,1)S(1)}, bf16[64,512]{1,0:T(8,128)(2,1)S(1)}, u32[]{:S(2)}, u32[]{:S(2)}) collective-permute-start(bf16[64,512]{1,0:T(8,128)(2,1)S(1)} %get-tuple-element.37), channel_id=1, source_target_pairs={{0,6},{1,27},{2,8},{3,29},{4,10},{5,31},{6,12},{7,1},{8,14},{9,3},... | collective-permute-start | bytes 196616 | tf_op jit(solution)/shard_map/ppermute | solution.py:28
  47.3 5.5 %collective-permute-start.11 = (bf16[256,512]{1,0:T(8,128)(2,1)S(1)}, bf16[256,512]{1,0:T(8,128)(2,1)S(1)}, u32[]{:S(2)}, u32[]{:S(2)}) collective-permute-start(bf16[256,512]{1,0:T(8,128)(2,1)S(1)} %constant_dynamic-update-slice_fusion.4.kept_ref), channel_id=1, source_target_pairs={{0,1},{1,0},{2,3},{3,2},{4,5},{5,4},{6,7},{7,6},{8,9},{9,8},{10,11... | collective-permute-start | bytes 786440 | tf_op jit(solution)/shard_map/ppermute | solution.py:32
  52.9 4.9 %copy-start.18 = (s32[8,128]{1,0:T(8,128)S(1)}, s32[8,128]{1,0:T(8,128)}, u32[]{:S(2)}) copy-start(s32[8,128]{1,0:T(8,128)} %rows_ref.5) | copy-start | bytes 12292
  57.2 2.8 %collective-permute-start.12 = (bf16[1024,512]{1,0:T(8,128)(2,1)S(1)}, bf16[1024,512]{1,0:T(8,128)(2,1)S(1)}, u32[]{:S(2)}, u32[]{:S(2)}) collective-permute-start(bf16[1024,512]{1,0:T(8,128)(2,1)S(1)} %get-tuple-element.38.part_ref), channel_id=1, source_target_pairs={{0,1},{1,0},{2,3},{3,2},{4,5},{5,4},{6,7},{7,6},{8,9},{9,8},{10,11... | collective-permute-start | bytes 3145736 | tf_op jit(solution)/shard_map/ppermute | solution.py:32
  57.7 2.3 %collective-permute-start = (s32[8,128]{1,0:T(8,128)S(1)}, s32[8,128]{1,0:T(8,128)S(1)}, u32[]{:S(2)}, u32[]{:S(2)}) collective-permute-start(s32[8,128]{1,0:T(8,128)S(1)} %copy-done.18), channel_id=1, source_target_pairs={{0,1},{1,0},{2,3},{3,2},{4,5},{5,4},{6,7},{7,6},{8,9},{9,8},{10,11... | collective-permute-start | bytes 12296 | tf_op jit(solution)/shard_map/ppermute | solution.py:32
  63.6 24.3 %copy-start.14 = (s32[512,8]{0,1:T(8,128)S(1)}, s32[512,8]{0,1:T(8,128)}, u32[]{:S(2)}) copy-start(s32[512,8]{0,1:T(8,128)} %param.21) | copy-start | bytes 49156
  63.6 24.3 %copy-start.15 = (f32[512,8]{0,1:T(8,128)S(1)}, f32[512,8]{0,1:T(8,128)}, u32[]{:S(2)}) copy-start(f32[512,8]{0,1:T(8,128)} %param.22) | copy-start | bytes 49156
  63.6 29.9 %copy-start.8 = (bf16[512,512]{1,0:T(8,128)(2,1)S(1)}, bf16[512,512]{1,0:T(8,128)(2,1)}, u32[]{:S(2)}) copy-start(bf16[512,512]{1,0:T(8,128)(2,1)} %embed_ref.1) | copy-start | bytes 1572868
  63.6 29.9 %copy-start.9 = (bf16[512,512]{1,0:T(8,128)(2,1)S(1)}, bf16[512,512]{1,0:T(8,128)(2,1)}, u32[]{:S(2)}) copy-start(bf16[512,512]{1,0:T(8,128)(2,1)} %first_ref.21) | copy-start | bytes 1572868
  63.6 29.9 %copy-start.19 = (bf16[4,512]{1,0:T(4,128)(2,1)S(1)}, bf16[4,512]{1,0:T(4,128)(2,1)}, u32[]{:S(2)}) copy-start(bf16[4,512]{1,0:T(4,128)(2,1)} %second_ref.9) | copy-start | bytes 12292
  63.6 12.9 %collective-permute-start.13 = (bf16[256,512]{1,0:T(8,128)(2,1)S(1)}, bf16[256,512]{1,0:T(8,128)(2,1)S(1)}, u32[]{:S(2)}, u32[]{:S(2)}) collective-permute-start(bf16[256,512]{1,0:T(8,128)(2,1)S(1)} %get-tuple-element.40), channel_id=1, source_target_pairs={{0,2},{1,31},{2,4},{3,1},{4,6},{5,3},{6,8},{7,5},{8,10},{9,7},{10,... | collective-permute-start | bytes 786440 | tf_op jit(solution)/shard_map/ppermute | solution.py:28
  64.7 11.8 %collective-permute-start.14 = (bf16[256,512]{1,0:T(8,128)(2,1)S(1)}, bf16[256,512]{1,0:T(8,128)(2,1)S(1)}, u32[]{:S(2)}, u32[]{:S(2)}) collective-permute-start(bf16[256,512]{1,0:T(8,128)(2,1)S(1)} %get-tuple-element.41), channel_id=1, source_target_pairs={{0,8},{1,25},{2,10},{3,27},{4,12},{5,29},{6,14},{7,31},{8,16},{9,1... | collective-permute-start | bytes 786440 | tf_op jit(solution)/shard_map/ppermute | solution.py:28
  64.7 23.0 %collective-permute-start.15 = (bf16[256,512]{1,0:T(8,128)(2,1)S(1)}, bf16[256,512]{1,0:T(8,128)(2,1)S(1)}, u32[]{:S(2)}, u32[]{:S(2)}) collective-permute-start(bf16[256,512]{1,0:T(8,128)(2,1)S(1)} %get-tuple-element.42), channel_id=1, source_target_pairs={{0,10},{1,23},{2,12},{3,25},{4,14},{5,27},{6,16},{7,29},{8,18},{9,... | collective-permute-start | bytes 786440 | tf_op jit(solution)/shard_map/ppermute | solution.py:28
  66.8 20.9 %collective-permute-start.16 = (bf16[256,512]{1,0:T(8,128)(2,1)S(1)}, bf16[256,512]{1,0:T(8,128)(2,1)S(1)}, u32[]{:S(2)}, u32[]{:S(2)}) collective-permute-start(bf16[256,512]{1,0:T(8,128)(2,1)S(1)} %get-tuple-element.43), channel_id=1, source_target_pairs={{0,6},{1,27},{2,8},{3,29},{4,10},{5,31},{6,12},{7,1},{8,14},{9,3},... | collective-permute-start | bytes 786440 | tf_op jit(solution)/shard_map/ppermute | solution.py:28
  87.8 5.7 %collective-permute-start.17 = (bf16[512,512]{1,0:T(8,128)(2,1)S(1)}, bf16[512,512]{1,0:T(8,128)(2,1)S(1)}, u32[]{:S(2)}, u32[]{:S(2)}) collective-permute-start(bf16[512,512]{1,0:T(8,128)(2,1)S(1)} %pad_maximum_fusion), channel_id=1, source_target_pairs={{0,1},{1,0},{2,3},{3,2},{4,5},{5,4},{6,7},{7,6},{8,9},{9,8},{10,11... | collective-permute-start | bytes 1572872 | tf_op jit(solution)/shard_map/ppermute | solution.py:32
where the time goes:
time: 95.9 us; the launch traced here: 95.6 us
  Pallas kernels  35 us (36%)
  waiting for transfers between devices  33 us (34%)
  starting transfers between devices  21.3 us (22%)
  local copies, waits for them, and re-layouts  5.33 us (6%)
  between operations  1 us (1%)
    pallas_call x13, Pallas kernels, run(): pl.pallas_call(kernel, in_specs=[SCALAR if a.ndim == 1 else ON_CHIP for a...  35 us
    ppermute x12, waiting for transfers between devices, both_ways(): return lax.ppermute(value, ('dom', 'feat'), pairs)  29.8 us
    ppermute x12, starting transfers between devices, both_ways(): return lax.ppermute(value, ('dom', 'feat'), pairs)  20.1 us
    unnamed x46, local copies, waits for them, and re-layouts  5.28 us
    ppermute x6, waiting for transfers between devices, swapped(): return lax.ppermute(value, 'feat', [(0, 1), (1, 0)])  3.16 us
  transfers between devices with their start and end apart: 18, of which 10 were waited for; matrix products, arithmetic and copies ran while one was open for 0% of the time, Pallas kernels for 19%

commit v1 on v0

v1 whole, which is shorter than its diff:
```python
import functools

import jax
import jax.numpy as jnp
from jax import lax
from jax.experimental import pallas as pl
from jax.experimental.pallas import tpu as pltpu
from jax.sharding import PartitionSpec as P

SPAN = 4
LANES = 128
CHUNK = 256
VMEM_GRANT = 24 << 20
HALO_ORDER = [2, 0, 3, 1]
PROBE_ORDER = [2, 3, 1, 0]
DIRECT = [0, 1]
SPLIT = [2, 3]
EARLY_FLOPS = 10**10
BF16 = jnp.bfloat16
F32 = jnp.float32


def offset_pairs(width):
    return [1, width, width + 1, width - 1]


def both_ways(value, steps):
    count = lax.axis_size("dom")
    pairs = []
    for source in range(count):
        pairs.append((2 * source, 2 * ((source + steps) % count)))
        pairs.append((2 * source + 1, 2 * ((source - steps) % count) + 1))
    return lax.ppermute(value, ("dom", "feat"), pairs)


def passed_along(value, steps):
    count = lax.axis_size("dom")
    return lax.ppermute(value, "dom", [(source, (source + steps) % count) for source in range(count)])


def swapped(value):
    return lax.ppermute(value, "feat", [(0, 1), (1, 0)])


def dot(left, right):
    return jnp.dot(left, right, preferred_element_type=F32)


def normed(values):
    shifted = values - jnp.mean(values, axis=-1, keepdims=True)
    spread = jnp.mean(shifted * shifted, axis=-1, keepdims=True)
    return shifted * lax.rsqrt(spread + 1e-05)


def columns_of(row):
    return jnp.broadcast_to(row, (LANES, row.shape[1])).T


def picks(columns, base, width):
    lane = lax.broadcasted_iota(jnp.int32, columns.shape, 1)
    parts = []
    for start in range(0, width, LANES):
        parts.append(jnp.where(columns == lane + (base + start), 1.0, 0.0).astype(BF16))
    return jnp.concatenate(parts, axis=1)


def index_columns(rows, first, count):
    per = rows.shape[1]
    parts = [columns_of(rows[r : r + 1, :]) for r in range(first // per, (first + count) // per)]
    return jnp.concatenate(parts, axis=0) if len(parts) > 1 else parts[0]


def chosen_rows(side, lists_ref, pair):
    even = lists_ref[pl.ds(2 * pair, 1), :]
    odd = lists_ref[pl.ds(2 * pair + 1, 1), :]
    return jnp.where(side == 0, even, odd)


def first_kernel(out_ref):
    out_ref[...] = jnp.zeros(out_ref.shape, out_ref.dtype)


def plan_kernel(rows_ref, far_rows_ref, plan_ref):
    side = lax.axis_index("feat")
    for pair in DIRECT:
        plan_ref[2 * pair : 2 * pair + 2, :] = rows_ref[2 * pair : 2 * pair + 2, :]
    for pair in SPLIT:
        plan_ref[2 * pair : 2 * pair + 1, :] = chosen_rows(side, rows_ref, pair)
        plan_ref[2 * pair + 1 : 2 * pair + 2, :] = chosen_rows(side, far_rows_ref, pair)


def halo_send_kernel(ready_ref, rows_ref, nodes_ref, *out_refs):
    for i, out_ref in enumerate(out_refs):
        row = chosen_rows(lax.axis_index("feat"), rows_ref, i)
        select = picks(columns_of(row), 0, nodes_ref.shape[0])
        out_ref[...] = dot(select, nodes_ref[...]).astype(BF16)


def edge_near_kernel(src_ref, dst_ref, nodes_ref, first_ref, near_ref, recv_ref, own_ref, *, layer):
    count, width = nodes_ref.shape
    own_ref[...] = dot(nodes_ref[...], first_ref[layer, width : 2 * width, :]).astype(BF16)
    recv_ref[...] = dot(nodes_ref[...], first_ref[layer, 2 * width : 3 * width, :]).astype(BF16)
    total_edges = near_ref.shape[0]
    src, dst = src_ref[...], dst_ref[...]
    for start in range(0, total_edges, CHUNK):
        total = dot(picks(index_columns(src, start, CHUNK), 0, count), own_ref[...])
        if start < total_edges // 2:
            total += dot(picks(index_columns(dst, start, CHUNK), 0, count), recv_ref[...])
        near_ref[start : start + CHUNK, :] = total


def edge_self_kernel(edges_ref, first_ref, self_ref, *, layer):
    self_ref[...] = dot(edges_ref[...], first_ref[layer, 0 : edges_ref.shape[1], :])


def halo_places(far, slot, side):
    block = lax.div(far, slot)
    place = lax.div(block, 2) * slot + lax.rem(far, slot)
    kept = lax.rem(block, 2) == side
    inside = far >= 0
    mine = jnp.where(jnp.logical_and(inside, kept), place, -1)
    others = jnp.where(jnp.logical_and(inside, jnp.logical_not(kept)), place, -1)
    return mine, others


def edge_kept_kernel(
    src_ref, dst_ref, self_ref, recv_ref, kept_ref, first_ref, mid_ref, table_ref, *, layer, slot
):
    side = lax.axis_index("feat")
    half, width = kept_ref.shape
    count = recv_ref.shape[0]
    total_edges = self_ref.shape[0]
    table_ref[...] = dot(kept_ref[...], first_ref[layer, width : 2 * width, :]).astype(BF16)
    mine, _ = halo_places(src_ref[...] - count, slot, side)
    dst = dst_ref[...]
    for start in range(0, total_edges, CHUNK):
        span = slice(start, start + CHUNK)
        total = self_ref[span, :] + dot(picks(index_columns(mine, start, CHUNK), 0, half), table_ref[...])
        if start >= total_edges // 2:
            total += dot(picks(index_columns(dst, start, CHUNK), 0, count), recv_ref[...])
        mid_ref[span, :] = total


def summed_rows(dst_ref, new_ref, out_ref, base):
    total_edges = new_ref.shape[0]
    for start in range(0, out_ref.shape[0], CHUNK):
        node = lax.broadcasted_iota(jnp.int32, (CHUNK, LANES), 0) + (base + start)
        parts = []
        for r in range(total_edges // LANES):
            row = jnp.broadcast_to(dst_ref[pl.ds(r, 1), :], (CHUNK, LANES))
            parts.append(jnp.where(row == node, 1.0, 0.0).astype(BF16))
        out_ref[start : start + CHUNK, :] = dot(jnp.concatenate(parts, axis=1), new_ref[...]).astype(BF16)


def edge_new_kernel(
    src_ref,
    dst_ref,
    near_ref,
    mid_ref,
    edges_ref,
    other_ref,
    first_ref,
    second_ref,
    new_ref,
    part_ref,
    table_ref,
    *,
    layer,
    slot,
    count,
):
    side = lax.axis_index("feat")
    half, width = other_ref.shape
    total_edges = edges_ref.shape[0]
    table_ref[...] = dot(other_ref[...], first_ref[layer, width : 2 * width, :]).astype(BF16)
    _, others = halo_places(src_ref[...] - count, slot, side)
    for start in range(0, total_edges, CHUNK):
        span = slice(start, start + CHUNK)
        hidden = near_ref[span, :] + mid_ref[span, :]
        hidden += dot(picks(index_columns(others, start, CHUNK), 0, half), table_ref[...])
        hidden = jnp.maximum(hidden, 0.0).astype(BF16)
        update = normed(dot(hidden, second_ref[layer]))
        new_ref[span, :] = (edges_ref[span, :].astype(F32) + update).astype(BF16)
    summed_rows(dst_ref, new_ref, part_ref, 0)


def edge_rest_kernel(dst_ref, new_ref, part_ref):
    summed_rows(dst_ref, new_ref, part_ref, part_ref.shape[0])


def node_own_kernel(rows_ref, nodes_ref, first_ref, own_ref, rows_own_ref, rows_nodes_ref, *, layer, direct):
    count, width = nodes_ref.shape
    top = first_ref[layer, 0:width, :]
    own_ref[...] = dot(nodes_ref[...], top)
    for i, columns in enumerate(send_columns(rows_ref, direct)):
        size = columns.shape[0]
        picked = dot(picks(columns, 0, count), nodes_ref[...]).astype(BF16)
        rows_nodes_ref[i * size : (i + 1) * size, :] = picked
    rows_own_ref[...] = dot(rows_nodes_ref[...], top)


def send_columns(rows_ref, direct):
    if direct is None:
        return [columns_of(chosen_rows(lax.axis_index("feat"), rows_ref, i)) for i in range(rows_ref.shape[0] // 2)]
    return [columns_of(rows_ref[pl.ds(k, 1), :]) for k in direct]


def node_update(nodes, own, summed, bottom, second):
    hidden = jnp.maximum(own + dot(summed, bottom), 0.0).astype(BF16)
    return (nodes.astype(F32) + normed(dot(hidden, second))).astype(BF16)


def node_send_kernel(
    rows_ref,
    part_a_ref,
    part_b_ref,
    other_a_ref,
    other_b_ref,
    rows_own_ref,
    rows_nodes_ref,
    first_ref,
    second_ref,
    summed_ref,
    *out_refs,
    layer,
    direct,
):
    count, width = summed_ref.shape
    half = count // 2
    summed_ref[0:half, :] = (part_a_ref[...].astype(F32) + other_a_ref[...].astype(F32)).astype(BF16)
    summed_ref[half:count, :] = (part_b_ref[...].astype(F32) + other_b_ref[...].astype(F32)).astype(BF16)
    bottom = first_ref[layer, width : 2 * width, :]
    second = second_ref[layer]
    columns = send_columns(rows_ref, direct)
    picked = jnp.concatenate([picks(c, 0, count) for c in columns], axis=0)
    picked = dot(picked, summed_ref[...]).astype(BF16)
    fresh = node_update(rows_nodes_ref[...], rows_own_ref[...], picked, bottom, second)
    for i, out_ref in enumerate(out_refs):
        size = out_ref.shape[0]
        out_ref[...] = fresh[i * size : (i + 1) * size, :]


def node_full_kernel(rows_ref, own_ref, summed_ref, nodes_ref, first_ref, second_ref, new_ref, *out_refs, layer, lists):
    count, width = nodes_ref.shape
    bottom = first_ref[layer, width : 2 * width, :]
    second = second_ref[layer]
    for start in range(0, count, CHUNK):
        span = slice(start, start + CHUNK)
        new_ref[span, :] = node_update(nodes_ref[span, :], own_ref[span, :], summed_ref[span, :], bottom, second)
    for picked, out_ref in zip(lists, out_refs):
        select = jnp.concatenate([picks(columns_of(rows_ref[pl.ds(k, 1), :]), 0, count) for k in picked], axis=0)
        out_ref[...] = dot(select, new_ref[...]).astype(BF16)


def weights_kernel(slots_ref, wgt_ref, out_ref, *, slot):
    side = lax.axis_index("feat")
    lane = lax.broadcasted_iota(jnp.int32, (LANES, LANES), 1)
    block = lax.div(slots_ref[...], slot)
    turn = lax.rem(block, 2)
    spot = jnp.zeros_like(block)
    for i, pair in enumerate(SPLIT):
        spot = jnp.where(lax.div(block, 2) == pair, jnp.where(turn == side, i, len(SPLIT) + i), spot)
    for i, pair in enumerate(DIRECT):
        spot = jnp.where(lax.div(block, 2) == pair, 2 * len(SPLIT) + 2 * i + turn, spot)
    spot = spot * slot + lax.rem(slots_ref[...], slot)
    for start in range(0, out_ref.shape[0], LANES):
        places = [columns_of(spot[k : k + 1, start : start + LANES]) for k in range(slots_ref.shape[0])]
        shares = [columns_of(wgt_ref[pl.ds(k, 1), start : start + LANES]) for k in range(slots_ref.shape[0])]
        for first in range(0, out_ref.shape[1], LANES):
            total = jnp.zeros((LANES, LANES), F32)
            for place, share in zip(places, shares):
                total += jnp.where(place == lane + first, share, 0.0)
            out_ref[start : start + LANES, first : first + LANES] = total.astype(BF16)


def interp_kernel(table_ref, embed_ref, *rest):
    *got_refs, out_ref = rest
    slot = table_ref.shape[1] // (2 * len(SPLIT) + 2 * len(DIRECT))
    total = embed_ref[...].astype(F32)
    for i, ref in enumerate(got_refs):
        at = i * slot if i < len(SPLIT) else (len(SPLIT) + i) * slot
        total += dot(table_ref[:, at : at + slot], ref[0:slot, :])
    out_ref[...] = total


def decode_kernel(table_ref, total_ref, other_ref, first_ref, second_ref, out_ref):
    half = other_ref.shape[0]
    total = total_ref[...] + dot(table_ref[:, half : 2 * half], other_ref[...])
    hidden = jnp.maximum(dot(total.astype(BF16), first_ref[...]), 0.0).astype(BF16)
    out_ref[...] = lax.dot_general(
        second_ref[...], hidden, (((1,), (1,)), ((), ())), preferred_element_type=F32
    )


SCALAR = pl.BlockSpec(memory_space=pltpu.SMEM)
ON_CHIP = pl.BlockSpec(memory_space=pltpu.VMEM)


def run(kernel, flops, outs, args, scratch=()):
    nbytes = sum(a.size * a.dtype.itemsize for a in args)
    return pl.pallas_call(
        kernel,
        in_specs=[SCALAR if a.ndim == 1 else ON_CHIP for a in args],
        out_specs=[SCALAR if len(shape) == 1 else ON_CHIP for shape, _ in outs],
        out_shape=[jax.ShapeDtypeStruct(shape, dtype) for shape, dtype in outs],
        scratch_shapes=list(scratch),
        compiler_params=pltpu.CompilerParams(vmem_limit_bytes=VMEM_GRANT),
        cost_estimate=pl.CostEstimate(flops=flops, bytes_accessed=nbytes, transcendentals=0),
    )(*args)


def body(
    node_lat,
    edge_lat,
    edge_src,
    edge_dst,
    halo_rows,
    probe_rows,
    probe_slot,
    probe_wgt,
    probe_embed,
    edge_first,
    edge_second,
    node_first,
    node_second,
    decode_first,
    decode_second,
):
    steps = offset_pairs(SPAN)
    pairs = len(steps)
    nodes, width = node_lat.shape
    edges = edge_lat.shape[0]
    slot = halo_rows.shape[1]
    qslot = probe_rows.shape[1]
    probes = probe_slot.shape[0]
    layers = edge_first.shape[0]
    half = pairs * slot
    square = 2 * width * width
    e = edge_lat
    h = node_lat
    src = edge_src.reshape(edges // LANES, LANES)
    dst = edge_dst.reshape(edges // LANES, LANES)
    (ready,) = run(first_kernel, EARLY_FLOPS, [((8, LANES), F32)], ())
    sends = run(halo_send_kernel, EARLY_FLOPS, [((slot, width), BF16)] * pairs, (ready, halo_rows, h))
    far_rows = swapped(probe_rows)
    node_full = None
    for layer in range(layers):
        last = layer + 1 == layers
        got = {}
        for i in HALO_ORDER:
            got[i] = both_ways(sends[i], steps[i])
        kept = jnp.concatenate([got[i] for i in range(pairs)], axis=0)
        if layer > 0:
            (h,) = node_full()
        near, recv = run(
            functools.partial(edge_near_kernel, layer=layer),
            2 * square * nodes + 3 * edges * nodes * width,
            [((edges, width), F32), ((nodes, width), BF16)],
            (src, dst, h, edge_first),
            [pltpu.VMEM((nodes, width), BF16)],
        )
        (self_part,) = run(
            functools.partial(edge_self_kernel, layer=layer), square * edges, [((edges, width), F32)], (e, edge_first)
        )
        if layer == 0:
            (plan,) = run(plan_kernel, 1000, [(probe_rows.shape, jnp.int32)], (probe_rows, far_rows))
        other = swapped(kept)
        (mid,) = run(
            functools.partial(edge_kept_kernel, layer=layer, slot=slot),
            square * half + 2 * half * edges * width + edges * nodes * width,
            [((edges, width), F32)],
            (src, dst, self_part, recv, kept, edge_first),
            [pltpu.VMEM((half, width), BF16)],
        )
        e, part_a = run(
            functools.partial(edge_new_kernel, layer=layer, slot=slot, count=nodes),
            square * (half + edges) + width * edges * (2 * half + nodes),
            [((edges, width), BF16), ((nodes // 2, width), BF16)],
            (src, dst, near, mid, e, other, edge_first, edge_second),
            [pltpu.VMEM((half, width), BF16)],
        )
        other_a = swapped(part_a)
        (part_b,) = run(edge_rest_kernel, width * edges * nodes, [((nodes // 2, width), BF16)], (dst, e))
        other_b = swapped(part_b)
        lists = plan if last else halo_rows
        direct = [2 * PROBE_ORDER[0], 2 * PROBE_ORDER[0] + 1] if last else None
        size = lists.shape[1]
        rows = 2 * size if last else half
        piece = rows if last and PROBE_ORDER[0] in SPLIT else size
        own, rows_own, rows_nodes = run(
            functools.partial(node_own_kernel, layer=layer, direct=direct),
            square * (nodes + rows) + 2 * rows * nodes * width,
            [((nodes, width), F32), ((rows, width), F32), ((rows, width), BF16)],
            (lists, h, node_first),
        )
        summed, *sends = run(
            functools.partial(node_send_kernel, layer=layer, direct=direct),
            2 * square * rows + 2 * rows * nodes * width,
            [((nodes, width), BF16)] + [((piece, width), BF16)] * (rows // piece),
            (lists, part_a, part_b, other_a, other_b, rows_own, rows_nodes, node_first, node_second),
        )
        picked = []
        for i in PROBE_ORDER[1:] if last else []:
            picked += [[2 * i], [2 * i + 1]] if i in DIRECT else [[2 * i, 2 * i + 1]]
        node_full = functools.partial(
            run,
            functools.partial(node_full_kernel, layer=layer, lists=picked),
            2 * square * nodes + 2 * sum(map(len, picked)) * size * nodes * width,
            [((nodes, width), BF16)] + [((len(p) * size, width), BF16) for p in picked],
            (lists, own, summed, h, node_first, node_second),
        )
    h, *rest = node_full()
    pieces = iter(list(sends) + rest)
    got = {}
    for i in PROBE_ORDER:
        for turn in range(2 if i in DIRECT else 1):
            if i in DIRECT:
                got[2 * i + turn] = passed_along(next(pieces), steps[i] * (1 - 2 * turn))
            else:
                got[2 * i] = both_ways(next(pieces), steps[i])
    kept = [got[2 * i] for i in SPLIT]
    ends = [got[2 * i + turn] for i in DIRECT for turn in range(2)]
    (table,) = run(
        functools.partial(weights_kernel, slot=qslot),
        48 * probes * pairs * qslot * pairs,
        [((probes, 2 * pairs * qslot), BF16)],
        (probe_slot.T, probe_wgt.T),
    )
    other = swapped(jnp.concatenate([piece[qslot:] for piece in kept], axis=0))
    (total,) = run(
        interp_kernel,
        2 * probes * width * (len(kept) + len(ends)) * qslot,
        [((probes, width), F32)],
        (table, probe_embed, *kept, *ends),
    )
    (fields,) = run(
        decode_kernel,
        2 * probes * width * (len(kept) * qslot + width),
        [((decode_second.shape[0], probes), F32)],
        (table, total, other, decode_first, decode_second),
    )
    return (h, fields)


def solution(mesh):
    return jax.shard_map(
        body,
        mesh=mesh,
        in_specs=(
            P("dom", None),
            P(("dom", "feat"), None),
            P(("dom", "feat")),
            P(("dom", "feat")),
            P("dom", None),
            P(("dom", "feat"), None),
            P(("dom", "feat"), None),
            P(("dom", "feat"), None),
            P(("dom", "feat"), None),
            P(),
            P(),
            P(),
            P(),
            P(),
            P(),
        ),
        out_specs=(P("dom", None), P(None, ("dom", "feat"))),
        check_vma=False,
    )
```

time: 95.9 us -> 90.1 us (0.940)
  waiting for transfers between devices: 33 us -> 25.1 us
  starting transfers between devices: 21.3 us -> 28.3 us
  local copies, waits for them, and re-layouts: 5.33 us -> 1.82 us
  Pallas kernels: 35 us -> 33.6 us
    ppermute x0 -> x4, starting transfers between devices: none -> 9.49 us  [passed_along(): lax.ppermute(value, 'dom', [(source, (source + steps) % count) for source...]
    ppermute x12 -> x10, waiting for transfers between devices: 29.8 us -> 21.8 us  [both_ways(): return lax.ppermute(value, ('dom', 'feat'), pairs)]
    unnamed x46 -> x36, local copies, waits for them, and re-layouts: 5.28 us -> 1.79 us
    ppermute x12 -> x10, starting transfers between devices: 20.1 us -> 17 us  [both_ways(): return lax.ppermute(value, ('dom', 'feat'), pairs)]
    ppermute x0 -> x4, waiting for transfers between devices: none -> 1.51 us  [passed_along(): lax.ppermute(value, 'dom', [(source, (source + steps) % count) for source...]
    ppermute x6 -> x8, waiting for transfers between devices: 3.16 us -> 1.8 us  [swapped(): return lax.ppermute(value, 'feat', [(0, 1), (1, 0)])]
    pallas_call x13 -> x22, Pallas kernels: 35 us -> 33.6 us  [run(): pl.pallas_call(kernel, in_specs=[SCALAR if a.ndim == 1 else ON_CHIP for a...]
  transfers between devices with their start and end apart: 18 -> 22, of which waited for: 10 -> 10; matrix products, arithmetic and copies ran while one was open for 0% -> 0% of each run, Pallas kernels for 19% -> 21%
where the time goes in v1:
time: 90.1 us; the launch traced here: 89.9 us
  Pallas kernels  33.6 us (37%)
  starting transfers between devices  28.3 us (31%)
  waiting for transfers between devices  25.1 us (28%)
  local copies, waits for them, and re-layouts  1.82 us (2%)
  between operations  1.07 us (1%)
    pallas_call x22, Pallas kernels, run(): pl.pallas_call(kernel, in_specs=[SCALAR if a.ndim == 1 else ON_CHIP for a...  33.6 us
    ppermute x10, waiting for transfers between devices, both_ways(): return lax.ppermute(value, ('dom', 'feat'), pairs)  21.8 us
    ppermute x10, starting transfers between devices, both_ways(): return lax.ppermute(value, ('dom', 'feat'), pairs)  17 us
    ppermute x4, starting transfers between devices, passed_along(): lax.ppermute(value, 'dom', [(source, (source + steps) % count) for source...  9.49 us
    ppermute x8, starting transfers between devices, swapped(): return lax.ppermute(value, 'feat', [(0, 1), (1, 0)])  1.84 us
  transfers between devices with their start and end apart: 22, of which 10 were waited for; matrix products, arithmetic and copies ran while one was open for 0% of the time, Pallas kernels for 21%

profile of v1, /device:TPU:0, one launch (start us, length us, event | category | flops | bytes accessed | tf_op | source)
XLA Modules:
  0.0 89.9 jit_solution(15824835875518635318)
XLA Ops:
  0.7 1.2 %copy-done.5 = bf16[1024,512]{1,0:T(8,128)(2,1)S(1)} copy-done((bf16[1024,512]{1,0:T(8,128)(2,1)S(1)}, bf16[1024,512]{1,0:T(8,128)(2,1)}, u32[]{:S(2)}) %copy-start.5) | copy-done | bytes 1048600
  1.9 0.9 shard_map.163
  2.8 3.0 %collective-permute-start.1 = (bf16[64,512]{1,0:T(8,128)(2,1)S(1)}, bf16[64,512]{1,0:T(8,128)(2,1)S(1)}, u32[]{:S(2)}, u32[]{:S(2)}) collective-permute-start(bf16[64,512]{1,0:T(8,128)(2,1)S(1)} %get-tuple-element.36), channel_id=1, source_target_pairs={{0,2},{1,31},{2,4},{3,1},{4,6},{5,3},{6,8},{7,5},{8,10},{9,7},{10,... | collective-permute-start | bytes 196616 | tf_op jit(solution)/shard_map/ppermute | solution.py:33
  5.8 1.6 %collective-permute-start.2 = (bf16[64,512]{1,0:T(8,128)(2,1)S(1)}, bf16[64,512]{1,0:T(8,128)(2,1)S(1)}, u32[]{:S(2)}, u32[]{:S(2)}) collective-permute-start(bf16[64,512]{1,0:T(8,128)(2,1)S(1)} %get-tuple-element.37), channel_id=1, source_target_pairs={{0,8},{1,25},{2,10},{3,27},{4,12},{5,29},{6,14},{7,31},{8,16},{9,1... | collective-permute-start | bytes 196616 | tf_op jit(solution)/shard_map/ppermute | solution.py:33
  7.4 2.5 %collective-permute-start.3 = (bf16[64,512]{1,0:T(8,128)(2,1)S(1)}, bf16[64,512]{1,0:T(8,128)(2,1)S(1)}, u32[]{:S(2)}, u32[]{:S(2)}) collective-permute-start(bf16[64,512]{1,0:T(8,128)(2,1)S(1)} %get-tuple-element.38), channel_id=1, source_target_pairs={{0,10},{1,23},{2,12},{3,25},{4,14},{5,27},{6,16},{7,29},{8,18},{9,... | collective-permute-start | bytes 196616 | tf_op jit(solution)/shard_map/ppermute | solution.py:33
  9.9 2.4 %collective-permute-start.4 = (bf16[64,512]{1,0:T(8,128)(2,1)S(1)}, bf16[64,512]{1,0:T(8,128)(2,1)S(1)}, u32[]{:S(2)}, u32[]{:S(2)}) collective-permute-start(bf16[64,512]{1,0:T(8,128)(2,1)S(1)} %get-tuple-element.39), channel_id=1, source_target_pairs={{0,6},{1,27},{2,8},{3,29},{4,10},{5,31},{6,12},{7,1},{8,14},{9,3},... | collective-permute-start | bytes 196616 | tf_op jit(solution)/shard_map/ppermute | solution.py:33
  12.3 0.7 shard_map.161.self_ref
  13.1 1.5 %collective-permute-done.3 = bf16[64,512]{1,0:T(8,128)(2,1)S(1)} collective-permute-done((bf16[64,512]{1,0:T(8,128)(2,1)S(1)}, bf16[64,512]{1,0:T(8,128)(2,1)S(1)}, u32[]{:S(2)}, u32[]{:S(2)}) %collective-permute-start.3) | collective-permute-done | bytes 65568 | tf_op jit(solution)/shard_map/ppermute | solution.py:33
  14.5 2.3 %collective-permute-done.4 = bf16[64,512]{1,0:T(8,128)(2,1)S(1)} collective-permute-done((bf16[64,512]{1,0:T(8,128)(2,1)S(1)}, bf16[64,512]{1,0:T(8,128)(2,1)S(1)}, u32[]{:S(2)}, u32[]{:S(2)}) %collective-permute-start.4) | collective-permute-done | bytes 65568 | tf_op jit(solution)/shard_map/ppermute | solution.py:33
  16.9 3.1 %shard_map.160 = (f32[1024,512]{1,0:T(8,128)S(1)}, bf16[1024,512]{1,0:T(8,128)(2,1)S(1)}) custom-call(s32[8,128]{1,0:T(8,128)S(1)} %bitcast.4, s32[8,128]{1,0:T(8,128)S(1)} %bitcast.10, bf16[1024,512]{1,0:T(8,128)(2,1)S(1)} %copy-done.5, bf16[2,1536,512]{2,1,0:T(8,128)(2,1)S(1)} %copy-done), custom_call_target="tpu_custom_call" | custom-call | flops 2684354560 | bytes 4202496 | tf_op jit(solution)/shard_map/pallas_call | solution.py:301
  20.0 1.4 %shard_map.164.mid_ref = f32[1024,512]{1,0:T(8,128)S(1)} custom-call(s32[8,128]{1,0:T(8,128)S(1)} %bitcast.5, s32[8,128]{1,0:T(8,128)S(1)} %bitcast.11, f32[1024,512]{1,0:T(8,128)S(1)} %shard_map.161.self_ref, bf16[1024,512]{1,0:T(8,128)(2,1)S(1)} %get-tuple-element.35.recv_ref, bf16[256,512]{1,0:T(8,128)(2,1)S(1)} %constant_dynamic-update-slice_fusion.kept_ref, ...), custom_call_target="tpu_custom_call" | custom-call | flops 939524096 | bytes 6561792 | tf_op jit(solution)/shard_map/pallas_call | solution.py:301
  21.4 2.5 %shard_map.165 = (bf16[1024,512]{1,0:T(8,128)(2,1)S(1)}, bf16[512,512]{1,0:T(8,128)(2,1)S(1)}) custom-call(s32[8,128]{1,0:T(8,128)S(1)} %bitcast.6, s32[8,128]{1,0:T(8,128)S(1)} %bitcast.12, f32[1024,512]{1,0:T(8,128)S(1)} %get-tuple-element.34.near_ref, f32[1024,512]{1,0:T(8,128)S(1)} %shard_map.164.mid_ref, bf16[1024,512]{1,0:T(8,128)(2,1)S(1)} %copy-done.3, ...), custom_call_target="tpu_custom_call" | custom-call | flops 1476395008 | bytes 9707520 | tf_op jit(solution)/shard_map/pallas_call | solution.py:301
  23.9 0.7 shard_map.166.part_b_ref
  24.6 0.6 collective-permute-start.7
  25.1 0.1 collective-permute-start.6
  25.2 1.6 %shard_map.159 = (f32[1024,512]{1,0:T(8,128)S(1)}, f32[256,512]{1,0:T(8,128)S(1)}, bf16[256,512]{1,0:T(8,128)(2,1)S(1)}) custom-call(s32[8,64]{1,0:T(8,128)S(1)} %copy-done.12, bf16[1024,512]{1,0:T(8,128)(2,1)S(1)} %copy-done.5, bf16[2,1024,512]{2,1,0:T(8,128)(2,1)S(1)} %copy-done.1), custom_call_target="tpu_custom_call" | custom-call | flops 939524096 | bytes 3147776 | tf_op jit(solution)/shard_map/pallas_call | solution.py:301
  26.8 0.7 shard_map.171.self_ref
  27.6 0.5 copy-done.2
  28.0 1.1 %shard_map.167 = (bf16[1024,512]{1,0:T(8,128)(2,1)S(1)}, bf16[64,512]{1,0:T(8,128)(2,1)S(1)}, bf16[64,512]{1,0:T(8,128)(2,1)S(1)}, bf16[64,512]{1,0:T(8,128)(2,1)S(1)}, bf16[64,512]{1,0:T(8,128)(2,1)S(1)}) custom-call(s32[8,64]{1,0:T(8,128)S(1)} %copy-done.12, bf16[512,512]{1,0:T(8,128)(2,1)S(1)} %get-tuple-element.40.part_a_ref, ...), custom_call_target="tpu_custom_call" | custom-call | flops 536870912 | bytes 6031360 | tf_op jit(solution)/shard_map/pallas_call | solution.py:301
  29.2 2.4 %collective-permute-start.8 = (bf16[64,512]{1,0:T(8,128)(2,1)S(1)}, bf16[64,512]{1,0:T(8,128)(2,1)S(1)}, u32[]{:S(2)}, u32[]{:S(2)}) collective-permute-start(bf16[64,512]{1,0:T(8,128)(2,1)S(1)} %get-tuple-element.48), channel_id=1, source_target_pairs={{0,2},{1,31},{2,4},{3,1},{4,6},{5,3},{6,8},{7,5},{8,10},{9,7},{10,... | collective-permute-start | bytes 196616 | tf_op jit(solution)/shard_map/ppermute | solution.py:33
  31.6 0.5 collective-permute-start.10
  32.2 2.9 %collective-permute-start.11 = (bf16[64,512]{1,0:T(8,128)(2,1)S(1)}, bf16[64,512]{1,0:T(8,128)(2,1)S(1)}, u32[]{:S(2)}, u32[]{:S(2)}) collective-permute-start(bf16[64,512]{1,0:T(8,128)(2,1)S(1)} %get-tuple-element.51), channel_id=1, source_target_pairs={{0,6},{1,27},{2,8},{3,29},{4,10},{5,31},{6,12},{7,1},{8,14},{9,3},... | collective-permute-start | bytes 196616 | tf_op jit(solution)/shard_map/ppermute | solution.py:33
  35.0 1.9 %shard_map.168.nodes_ref = bf16[1024,512]{1,0:T(8,128)(2,1)S(1)} custom-call(s32[8,64]{1,0:T(8,128)S(1)} %copy-done.12, f32[1024,512]{1,0:T(8,128)S(1)} %get-tuple-element.33.own_ref, bf16[1024,512]{1,0:T(8,128)(2,1)S(1)} %get-tuple-element.44.summed_ref, bf16[1024,512]{1,0:T(8,128)(2,1)S(1)} %copy-done.5, bf16[2,1024,512]{2,1,0:T(8,128)(2,1)S(1)} %copy-done.1, ...), custom_call_target="tpu_custom_call" | custom-call | flops 1073741824 | bytes 7342080 | tf_op jit(solution)/shard_map/pallas_call | solution.py:301
  36.9 0.8 collective-permute-done.8
  37.7 0.3 collective-permute-done.9
  38.0 3.0 %collective-permute-done.10 = bf16[64,512]{1,0:T(8,128)(2,1)S(1)} collective-permute-done((bf16[64,512]{1,0:T(8,128)(2,1)S(1)}, bf16[64,512]{1,0:T(8,128)(2,1)S(1)}, u32[]{:S(2)}, u32[]{:S(2)}) %collective-permute-start.10) | collective-permute-done | bytes 65568 | tf_op jit(solution)/shard_map/ppermute | solution.py:33
  41.1 3.1 %shard_map.170 = (f32[1024,512]{1,0:T(8,128)S(1)}, bf16[1024,512]{1,0:T(8,128)(2,1)S(1)}) custom-call(s32[8,128]{1,0:T(8,128)S(1)} %bitcast.7, s32[8,128]{1,0:T(8,128)S(1)} %bitcast.14, bf16[1024,512]{1,0:T(8,128)(2,1)S(1)} %shard_map.168.nodes_ref, bf16[2,1536,512]{2,1,0:T(8,128)(2,1)S(1)} %copy-done), custom_call_target="tpu_custom_call" | custom-call | flops 2684354560 | bytes 4202496 | tf_op jit(solution)/shard_map/pallas_call | solution.py:301
  44.2 1.4 %shard_map.172.mid_ref = f32[1024,512]{1,0:T(8,128)S(1)} custom-call(s32[8,128]{1,0:T(8,128)S(1)} %bitcast.8, s32[8,128]{1,0:T(8,128)S(1)} %bitcast.15, f32[1024,512]{1,0:T(8,128)S(1)} %shard_map.171.self_ref, bf16[1024,512]{1,0:T(8,128)(2,1)S(1)} %get-tuple-element.47.recv_ref, bf16[256,512]{1,0:T(8,128)(2,1)S(1)} %constant_dynamic-update-slice_fusion.4.kept_ref, ...), custom_call_target="tpu_custom_call" | custom-call | flops 939524096 | bytes 6561792 | tf_op jit(solution)/shard_map/pallas_call | solution.py:301
  45.6 2.5 %shard_map.173 = (bf16[1024,512]{1,0:T(8,128)(2,1)S(1)}, bf16[512,512]{1,0:T(8,128)(2,1)S(1)}) custom-call(s32[8,128]{1,0:T(8,128)S(1)} %bitcast.9, s32[8,128]{1,0:T(8,128)S(1)} %bitcast.16, f32[1024,512]{1,0:T(8,128)S(1)} %get-tuple-element.46.near_ref, f32[1024,512]{1,0:T(8,128)S(1)} %shard_map.172.mid_ref, ...), custom_call_target="tpu_custom_call" | custom-call | flops 1476395008 | bytes 9707520 | tf_op jit(solution)/shard_map/pallas_call | solution.py:301
  48.1 0.7 shard_map.174.part_b_ref
  48.8 0.6 collective-permute-start.14
  49.4 0.1 collective-permute-start.13
  49.4 0.4 collective-permute-start
  49.9 1.8 %collective-permute-done.far_rows_ref = s32[8,128]{1,0:T(8,128)S(1)} collective-permute-done((s32[8,128]{1,0:T(8,128)S(1)}, s32[8,128]{1,0:T(8,128)S(1)}, u32[]{:S(2)}, u32[]{:S(2)}) %collective-permute-start) | collective-permute-done | bytes 4128 | tf_op jit(solution)/shard_map/ppermute | solution.py:42
  51.7 1.2 %shard_map.169 = (f32[1024,512]{1,0:T(8,128)S(1)}, f32[256,512]{1,0:T(8,128)S(1)}, bf16[256,512]{1,0:T(8,128)(2,1)S(1)}) custom-call(s32[8,128]{1,0:T(8,128)S(1)} %shard_map.158.rows_ref, bf16[1024,512]{1,0:T(8,128)(2,1)S(1)} %shard_map.168.nodes_ref, bf16[2,1024,512]{2,1,0:T(8,128)(2,1)S(1)} %copy-done.1), custom_call_target="tpu_custom_call" | custom-call | flops 939524096 | bytes 3149824 | tf_op jit(solution)/shard_map/pallas_call | solution.py:301
  52.9 1.1 %shard_map.175 = (bf16[1024,512]{1,0:T(8,128)(2,1)S(1)}, bf16[256,512]{1,0:T(8,128)(2,1)S(1)}) custom-call(s32[8,128]{1,0:T(8,128)S(1)} %shard_map.158.rows_ref, bf16[512,512]{1,0:T(8,128)(2,1)S(1)} %get-tuple-element.52.part_a_ref, bf16[512,512]{1,0:T(8,128)(2,1)S(1)} %shard_map.174.part_b_ref, bf16[512,512]{1,0:T(8,128)(2,1)S(1)} %collective-permute-done.13.other_a_ref, ...), custom_call_target="tpu_custom_call" | custom-call | flops 536870912 | bytes 6033408 | tf_op jit(solution)/shard_map/pallas_call | solution.py:301
  54.1 3.5 %shard_map.176 = (bf16[1024,512]{1,0:T(8,128)(2,1)}, bf16[256,512]{1,0:T(8,128)(2,1)S(1)}, bf16[128,512]{1,0:T(8,128)(2,1)S(1)}, bf16[128,512]{1,0:T(8,128)(2,1)...) custom-call(s32[8,128]{1,0:T(8,128)S(1)} %shard_map.158.rows_ref, ...), custom_call_target="tpu_custom_call" | custom-call | flops 1879048192 | bytes 7344128 | tf_op jit(solution)/shard_map/pallas_call | solution.py:301
  57.5 1.6 %collective-permute-start.15 = (bf16[256,512]{1,0:T(8,128)(2,1)S(1)}, bf16[256,512]{1,0:T(8,128)(2,1)S(1)}, u32[]{:S(2)}, u32[]{:S(2)}) collective-permute-start(bf16[256,512]{1,0:T(8,128)(2,1)S(1)} %get-tuple-element.58), channel_id=1, source_target_pairs={{0,10},{1,23},{2,12},{3,25},{4,14},{5,27},{6,16},{7,29},{8,18},{9,... | collective-permute-start | bytes 786440 | tf_op jit(solution)/shard_map/ppermute | solution.py:33
  59.1 10.3 %collective-permute-done.16.rest_1_ = bf16[256,512]{1,0:T(8,128)(2,1)S(1)} collective-permute-done((bf16[256,512]{1,0:T(8,128)(2,1)S(1)}, bf16[256,512]{1,0:T(8,128)(2,1)S(1)}, u32[]{:S(2)}, u32[]{:S(2)}) %collective-permute-start.16) | collective-permute-done | bytes 262176 | tf_op jit(solution)/shard_map/ppermute | solution.py:33
  69.4 3.7 %collective-permute-done.15.rest_0_ = bf16[256,512]{1,0:T(8,128)(2,1)S(1)} collective-permute-done((bf16[256,512]{1,0:T(8,128)(2,1)S(1)}, bf16[256,512]{1,0:T(8,128)(2,1)S(1)}, u32[]{:S(2)}, u32[]{:S(2)}) %collective-permute-start.15) | collective-permute-done | bytes 262176 | tf_op jit(solution)/shard_map/ppermute | solution.py:33
  73.1 0.1 collective-permute-start.21
  73.2 5.6 %collective-permute-start.18 = (bf16[128,512]{1,0:T(8,128)(2,1)S(1)}, bf16[128,512]{1,0:T(8,128)(2,1)S(1)}, u32[]{:S(2)}, u32[]{:S(2)}) collective-permute-start(bf16[128,512]{1,0:T(8,128)(2,1)S(1)} %get-tuple-element.61), channel_id=1, source_target_pairs={{0,30},{2,0},{4,2},{6,4},{8,6},{10,8},{12,10},{14,12},{16,14},{18,... | collective-permute-start | bytes 393224 | tf_op jit(solution)/shard_map/ppermute | solution.py:38
  78.9 3.8 %collective-permute-start.20 = (bf16[128,512]{1,0:T(8,128)(2,1)S(1)}, bf16[128,512]{1,0:T(8,128)(2,1)S(1)}, u32[]{:S(2)}, u32[]{:S(2)}) collective-permute-start(bf16[128,512]{1,0:T(8,128)(2,1)S(1)} %get-tuple-element.63), channel_id=1, source_target_pairs={{0,24},{2,26},{4,28},{6,30},{8,0},{10,2},{12,4},{14,6},{16,8},{18,... | collective-permute-start | bytes 393224 | tf_op jit(solution)/shard_map/ppermute | solution.py:38
  82.7 3.3 %shard_map.177.table_ref = bf16[512,1024]{1,0:T(8,128)(2,1)S(1)} custom-call(s32[8,512]{1,0:T(8,128)S(1)} %bitcast.18, f32[8,512]{1,0:T(8,128)S(1)} %bitcast.19), custom_call_target="tpu_custom_call" | custom-call | flops 50331648 | bytes 32768 | tf_op jit(solution)/shard_map/pallas_call | solution.py:301
  86.1 1.0 %collective-permute-done.19.rest_4_ = bf16[128,512]{1,0:T(8,128)(2,1)S(1)} collective-permute-done((bf16[128,512]{1,0:T(8,128)(2,1)S(1)}, bf16[128,512]{1,0:T(8,128)(2,1)S(1)}, u32[]{:S(2)}, u32[]{:S(2)}) %collective-permute-start.19) | collective-permute-done | bytes 131104 | tf_op jit(solution)/shard_map/ppermute | solution.py:38
  87.0 0.5 collective-permute-done.20.rest_5_
  87.6 1.0 %shard_map.178.total_ref = f32[512,512]{1,0:T(8,128)S(1)} custom-call(bf16[512,1024]{1,0:T(8,128)(2,1)S(1)} %shard_map.177.table_ref, bf16[512,512]{1,0:T(8,128)(2,1)S(1)} %copy-done.6, bf16[256,512]{1,0:T(8,128)(2,1)S(1)} %collective-permute-done.15.rest_0_, bf16[256,512]{1,0:T(8,128)(2,1)S(1)} %collective-permute-done.16.rest_1_, ...), custom_call_target="tpu_custom_call" | custom-call | flops 402653184 | bytes 2621440 | tf_op jit(solution)/shard_map/pallas_call | solution.py:301
  88.6 1.4 %shard_map.179 = f32[4,512]{1,0:T(4,128)} custom-call(bf16[512,1024]{1,0:T(8,128)(2,1)S(1)} %shard_map.177.table_ref, f32[512,512]{1,0:T(8,128)S(1)} %shard_map.178.total_ref, bf16[256,512]{1,0:T(8,128)(2,1)S(1)} %collective-permute-done.21.other_ref, bf16[512,512]{1,0:T(8,128)(2,1)S(1)} %copy-done.7, bf16[4,512]{1,0:T(4,128)(2,1)S(1)} %copy-done.13), custom_call_target="tpu_custom_call" | custom-call | flops 402653184 | bytes 2887680 | tf_op jit(solution)/shard_map/pallas_call | solution.py:301
  (59 shorter events, 0.4 us)
Async XLA Ops:
  0.6 1.2 %copy-start.5 = (bf16[1024,512]{1,0:T(8,128)(2,1)S(1)}, bf16[1024,512]{1,0:T(8,128)(2,1)}, u32[]{:S(2)}) copy-start(bf16[1024,512]{1,0:T(8,128)(2,1)} %nodes_ref.7) | copy-start | bytes 3145732
  0.6 1.2 %copy-start.12 = (s32[8,64]{1,0:T(8,128)S(1)}, s32[8,64]{1,0:T(8,128)}, u32[]{:S(2)}) copy-start(s32[8,64]{1,0:T(8,128)} %rows_ref.9) | copy-start | bytes 6148
  1.9 10.5 %copy-start = (bf16[2,1536,512]{2,1,0:T(8,128)(2,1)S(1)}, bf16[2,1536,512]{2,1,0:T(8,128)(2,1)}, u32[]{:S(2)}) copy-start(bf16[2,1536,512]{2,1,0:T(8,128)(2,1)} %first_ref.26) | copy-start | bytes 9437188
  1.9 10.5 %copy-start.3 = (bf16[1024,512]{1,0:T(8,128)(2,1)S(1)}, bf16[1024,512]{1,0:T(8,128)(2,1)}, u32[]{:S(2)}) copy-start(bf16[1024,512]{1,0:T(8,128)(2,1)} %edges_ref.3) | copy-start | bytes 3145732
  2.8 10.3 %collective-permute-start.1 = (bf16[64,512]{1,0:T(8,128)(2,1)S(1)}, bf16[64,512]{1,0:T(8,128)(2,1)S(1)}, u32[]{:S(2)}, u32[]{:S(2)}) collective-permute-start(bf16[64,512]{1,0:T(8,128)(2,1)S(1)} %get-tuple-element.36), channel_id=1, source_target_pairs={{0,2},{1,31},{2,4},{3,1},{4,6},{5,3},{6,8},{7,5},{8,10},{9,7},{10,... | collective-permute-start | bytes 196616 | tf_op jit(solution)/shard_map/ppermute | solution.py:33
  5.8 7.3 %collective-permute-start.2 = (bf16[64,512]{1,0:T(8,128)(2,1)S(1)}, bf16[64,512]{1,0:T(8,128)(2,1)S(1)}, u32[]{:S(2)}, u32[]{:S(2)}) collective-permute-start(bf16[64,512]{1,0:T(8,128)(2,1)S(1)} %get-tuple-element.37), channel_id=1, source_target_pairs={{0,8},{1,25},{2,10},{3,27},{4,12},{5,29},{6,14},{7,31},{8,16},{9,1... | collective-permute-start | bytes 196616 | tf_op jit(solution)/shard_map/ppermute | solution.py:33
  7.4 7.2 %collective-permute-start.3 = (bf16[64,512]{1,0:T(8,128)(2,1)S(1)}, bf16[64,512]{1,0:T(8,128)(2,1)S(1)}, u32[]{:S(2)}, u32[]{:S(2)}) collective-permute-start(bf16[64,512]{1,0:T(8,128)(2,1)S(1)} %get-tuple-element.38), channel_id=1, source_target_pairs={{0,10},{1,23},{2,12},{3,25},{4,14},{5,27},{6,16},{7,29},{8,18},{9,... | collective-permute-start | bytes 196616 | tf_op jit(solution)/shard_map/ppermute | solution.py:33
  9.9 7.0 %copy-start.8 = (s32[1024]{0:T(1024)S(1)}, s32[1024]{0:T(1024)}, u32[]{:S(2)}) copy-start(s32[1024]{0:T(1024)} %param.17) | copy-start | bytes 12292
  9.9 7.0 %copy-start.9 = (s32[1024]{0:T(1024)S(1)}, s32[1024]{0:T(1024)}, u32[]{:S(2)}) copy-start(s32[1024]{0:T(1024)} %param.18) | copy-start | bytes 12292
  9.9 7.0 %collective-permute-start.4 = (bf16[64,512]{1,0:T(8,128)(2,1)S(1)}, bf16[64,512]{1,0:T(8,128)(2,1)S(1)}, u32[]{:S(2)}, u32[]{:S(2)}) collective-permute-start(bf16[64,512]{1,0:T(8,128)(2,1)S(1)} %get-tuple-element.39), channel_id=1, source_target_pairs={{0,6},{1,27},{2,8},{3,29},{4,10},{5,31},{6,12},{7,1},{8,14},{9,3},... | collective-permute-start | bytes 196616 | tf_op jit(solution)/shard_map/ppermute | solution.py:33
  16.8 4.5 %collective-permute-start.5 = (bf16[256,512]{1,0:T(8,128)(2,1)S(1)}, bf16[256,512]{1,0:T(8,128)(2,1)S(1)}, u32[]{:S(2)}, u32[]{:S(2)}) collective-permute-start(bf16[256,512]{1,0:T(8,128)(2,1)S(1)} %constant_dynamic-update-slice_fusion.kept_ref), channel_id=1, source_target_pairs={{0,1},{1,0},{2,3},{3,2},{4,5},{5,4},{6,7},{7,6},{8,9},{9,8},{10,11... | collective-permute-start | bytes 786440 | tf_op jit(solution)/shard_map/ppermute | solution.py:42
  20.0 1.4 %copy-start.4 = (bf16[2,512,512]{2,1,0:T(8,128)(2,1)S(1)}, bf16[2,512,512]{2,1,0:T(8,128)(2,1)}, u32[]{:S(2)}) copy-start(bf16[2,512,512]{2,1,0:T(8,128)(2,1)} %second_ref.10) | copy-start | bytes 3145732
  21.4 3.8 %copy-start.1 = (bf16[2,1024,512]{2,1,0:T(8,128)(2,1)S(1)}, bf16[2,1024,512]{2,1,0:T(8,128)(2,1)}, u32[]{:S(2)}) copy-start(bf16[2,1024,512]{2,1,0:T(8,128)(2,1)} %first_ref.28) | copy-start | bytes 6291460
  24.6 2.9 %collective-permute-start.7 = (bf16[512,512]{1,0:T(8,128)(2,1)S(1)}, bf16[512,512]{1,0:T(8,128)(2,1)S(1)}, u32[]{:S(2)}, u32[]{:S(2)}) collective-permute-start(bf16[512,512]{1,0:T(8,128)(2,1)S(1)} %shard_map.166.part_b_ref), channel_id=1, source_target_pairs={{0,1},{1,0},{2,3},{3,2},{4,5},{5,4},{6,7},{7,6},{8,9},{9,8},{10,11... | collective-permute-start | bytes 1572872 | tf_op jit(solution)/shard_map/ppermute | solution.py:42
  25.1 2.4 %collective-permute-start.6 = (bf16[512,512]{1,0:T(8,128)(2,1)S(1)}, bf16[512,512]{1,0:T(8,128)(2,1)S(1)}, u32[]{:S(2)}, u32[]{:S(2)}) collective-permute-start(bf16[512,512]{1,0:T(8,128)(2,1)S(1)} %get-tuple-element.40.part_a_ref), channel_id=1, source_target_pairs={{0,1},{1,0},{2,3},{3,2},{4,5},{5,4},{6,7},{7,6},{8,9},{9,8},{10,11... | collective-permute-start | bytes 1572872 | tf_op jit(solution)/shard_map/ppermute | solution.py:42
  26.8 1.2 %copy-start.2 = (bf16[2,512,512]{2,1,0:T(8,128)(2,1)S(1)}, bf16[2,512,512]{2,1,0:T(8,128)(2,1)}, u32[]{:S(2)}) copy-start(bf16[2,512,512]{2,1,0:T(8,128)(2,1)} %second_ref.12) | copy-start | bytes 3145732
  29.2 8.5 %collective-permute-start.8 = (bf16[64,512]{1,0:T(8,128)(2,1)S(1)}, bf16[64,512]{1,0:T(8,128)(2,1)S(1)}, u32[]{:S(2)}, u32[]{:S(2)}) collective-permute-start(bf16[64,512]{1,0:T(8,128)(2,1)S(1)} %get-tuple-element.48), channel_id=1, source_target_pairs={{0,2},{1,31},{2,4},{3,1},{4,6},{5,3},{6,8},{7,5},{8,10},{9,7},{10,... | collective-permute-start | bytes 196616 | tf_op jit(solution)/shard_map/ppermute | solution.py:33
  31.6 6.4 %collective-permute-start.9 = (bf16[64,512]{1,0:T(8,128)(2,1)S(1)}, bf16[64,512]{1,0:T(8,128)(2,1)S(1)}, u32[]{:S(2)}, u32[]{:S(2)}) collective-permute-start(bf16[64,512]{1,0:T(8,128)(2,1)S(1)} %get-tuple-element.49), channel_id=1, source_target_pairs={{0,8},{1,25},{2,10},{3,27},{4,12},{5,29},{6,14},{7,31},{8,16},{9,1... | collective-permute-start | bytes 196616 | tf_op jit(solution)/shard_map/ppermute | solution.py:33
  31.6 9.4 %collective-permute-start.10 = (bf16[64,512]{1,0:T(8,128)(2,1)S(1)}, bf16[64,512]{1,0:T(8,128)(2,1)S(1)}, u32[]{:S(2)}, u32[]{:S(2)}) collective-permute-start(bf16[64,512]{1,0:T(8,128)(2,1)S(1)} %get-tuple-element.50), channel_id=1, source_target_pairs={{0,10},{1,23},{2,12},{3,25},{4,14},{5,27},{6,16},{7,29},{8,18},{9,... | collective-permute-start | bytes 196616 | tf_op jit(solution)/shard_map/ppermute | solution.py:33
  32.2 8.8 %collective-permute-start.11 = (bf16[64,512]{1,0:T(8,128)(2,1)S(1)}, bf16[64,512]{1,0:T(8,128)(2,1)S(1)}, u32[]{:S(2)}, u32[]{:S(2)}) collective-permute-start(bf16[64,512]{1,0:T(8,128)(2,1)S(1)} %get-tuple-element.51), channel_id=1, source_target_pairs={{0,6},{1,27},{2,8},{3,29},{4,10},{5,31},{6,12},{7,1},{8,14},{9,3},... | collective-permute-start | bytes 196616 | tf_op jit(solution)/shard_map/ppermute | solution.py:33
  41.0 4.6 %collective-permute-start.12 = (bf16[256,512]{1,0:T(8,128)(2,1)S(1)}, bf16[256,512]{1,0:T(8,128)(2,1)S(1)}, u32[]{:S(2)}, u32[]{:S(2)}) collective-permute-start(bf16[256,512]{1,0:T(8,128)(2,1)S(1)} %constant_dynamic-update-slice_fusion.4.kept_ref), channel_id=1, source_target_pairs={{0,1},{1,0},{2,3},{3,2},{4,5},{5,4},{6,7},{7,6},{8,9},{9,8},{10,11... | collective-permute-start | bytes 786440 | tf_op jit(solution)/shard_map/ppermute | solution.py:42
  45.6 3.9 %copy-start.14 = (s32[8,128]{1,0:T(8,128)S(1)}, s32[8,128]{1,0:T(8,128)}, u32[]{:S(2)}) copy-start(s32[8,128]{1,0:T(8,128)} %rows_ref.5) | copy-start | bytes 12292
  48.8 4.0 %collective-permute-start.14 = (bf16[512,512]{1,0:T(8,128)(2,1)S(1)}, bf16[512,512]{1,0:T(8,128)(2,1)S(1)}, u32[]{:S(2)}, u32[]{:S(2)}) collective-permute-start(bf16[512,512]{1,0:T(8,128)(2,1)S(1)} %shard_map.174.part_b_ref), channel_id=1, source_target_pairs={{0,1},{1,0},{2,3},{3,2},{4,5},{5,4},{6,7},{7,6},{8,9},{9,8},{10,11... | collective-permute-start | bytes 1572872 | tf_op jit(solution)/shard_map/ppermute | solution.py:42
  49.4 3.5 %collective-permute-start.13 = (bf16[512,512]{1,0:T(8,128)(2,1)S(1)}, bf16[512,512]{1,0:T(8,128)(2,1)S(1)}, u32[]{:S(2)}, u32[]{:S(2)}) collective-permute-start(bf16[512,512]{1,0:T(8,128)(2,1)S(1)} %get-tuple-element.52.part_a_ref), channel_id=1, source_target_pairs={{0,1},{1,0},{2,3},{3,2},{4,5},{5,4},{6,7},{7,6},{8,9},{9,8},{10,11... | collective-permute-start | bytes 1572872 | tf_op jit(solution)/shard_map/ppermute | solution.py:42
  49.4 2.2 %collective-permute-start = (s32[8,128]{1,0:T(8,128)S(1)}, s32[8,128]{1,0:T(8,128)S(1)}, u32[]{:S(2)}, u32[]{:S(2)}) collective-permute-start(s32[8,128]{1,0:T(8,128)S(1)} %copy-done.14), channel_id=1, source_target_pairs={{0,1},{1,0},{2,3},{3,2},{4,5},{5,4},{6,7},{7,6},{8,9},{9,8},{10,11... | collective-permute-start | bytes 12296 | tf_op jit(solution)/shard_map/ppermute | solution.py:42
  54.0 28.7 %copy-start.10 = (s32[512,8]{0,1:T(8,128)S(1)}, s32[512,8]{0,1:T(8,128)}, u32[]{:S(2)}) copy-start(s32[512,8]{0,1:T(8,128)} %param.21) | copy-start | bytes 49156
  54.0 28.6 %copy-start.11 = (f32[512,8]{0,1:T(8,128)S(1)}, f32[512,8]{0,1:T(8,128)}, u32[]{:S(2)}) copy-start(f32[512,8]{0,1:T(8,128)} %param.22) | copy-start | bytes 49156
  57.5 30.1 %copy-start.6 = (bf16[512,512]{1,0:T(8,128)(2,1)S(1)}, bf16[512,512]{1,0:T(8,128)(2,1)}, u32[]{:S(2)}) copy-start(bf16[512,512]{1,0:T(8,128)(2,1)} %embed_ref.1) | copy-start | bytes 1572868
  57.5 11.9 %collective-permute-start.16 = (bf16[256,512]{1,0:T(8,128)(2,1)S(1)}, bf16[256,512]{1,0:T(8,128)(2,1)S(1)}, u32[]{:S(2)}, u32[]{:S(2)}) collective-permute-start(bf16[256,512]{1,0:T(8,128)(2,1)S(1)} %get-tuple-element.59), channel_id=1, source_target_pairs={{0,6},{1,27},{2,8},{3,29},{4,10},{5,31},{6,12},{7,1},{8,14},{9,3},... | collective-permute-start | bytes 786440 | tf_op jit(solution)/shard_map/ppermute | solution.py:33
  57.5 15.5 %collective-permute-start.15 = (bf16[256,512]{1,0:T(8,128)(2,1)S(1)}, bf16[256,512]{1,0:T(8,128)(2,1)S(1)}, u32[]{:S(2)}, u32[]{:S(2)}) collective-permute-start(bf16[256,512]{1,0:T(8,128)(2,1)S(1)} %get-tuple-element.58), channel_id=1, source_target_pairs={{0,10},{1,23},{2,12},{3,25},{4,14},{5,27},{6,16},{7,29},{8,18},{9,... | collective-permute-start | bytes 786440 | tf_op jit(solution)/shard_map/ppermute | solution.py:33
  73.1 15.4 %collective-permute-start.21 = (bf16[256,512]{1,0:T(8,128)(2,1)S(1)}, bf16[256,512]{1,0:T(8,128)(2,1)S(1)}, u32[]{:S(2)}, u32[]{:S(2)}) collective-permute-start(bf16[256,512]{1,0:T(8,128)(2,1)S(1)} %pad_maximum_fusion), channel_id=1, source_target_pairs={{0,1},{1,0},{2,3},{3,2},{4,5},{5,4},{6,7},{7,6},{8,9},{9,8},{10,11... | collective-permute-start | bytes 786440 | tf_op jit(solution)/shard_map/ppermute | solution.py:42
  73.2 12.9 %collective-permute-start.17 = (bf16[128,512]{1,0:T(8,128)(2,1)S(1)}, bf16[128,512]{1,0:T(8,128)(2,1)S(1)}, u32[]{:S(2)}, u32[]{:S(2)}) collective-permute-start(bf16[128,512]{1,0:T(8,128)(2,1)S(1)} %get-tuple-element.60), channel_id=1, source_target_pairs={{0,2},{2,4},{4,6},{6,8},{8,10},{10,12},{12,14},{14,16},{16,18},{18... | collective-permute-start | bytes 393224 | tf_op jit(solution)/shard_map/ppermute | solution.py:38
  73.2 12.8 %collective-permute-start.18 = (bf16[128,512]{1,0:T(8,128)(2,1)S(1)}, bf16[128,512]{1,0:T(8,128)(2,1)S(1)}, u32[]{:S(2)}, u32[]{:S(2)}) collective-permute-start(bf16[128,512]{1,0:T(8,128)(2,1)S(1)} %get-tuple-element.61), channel_id=1, source_target_pairs={{0,30},{2,0},{4,2},{6,4},{8,6},{10,8},{12,10},{14,12},{16,14},{18,... | collective-permute-start | bytes 393224 | tf_op jit(solution)/shard_map/ppermute | solution.py:38
  78.9 8.2 %collective-permute-start.19 = (bf16[128,512]{1,0:T(8,128)(2,1)S(1)}, bf16[128,512]{1,0:T(8,128)(2,1)S(1)}, u32[]{:S(2)}, u32[]{:S(2)}) collective-permute-start(bf16[128,512]{1,0:T(8,128)(2,1)S(1)} %get-tuple-element.62), channel_id=1, source_target_pairs={{0,8},{2,10},{4,12},{6,14},{8,16},{10,18},{12,20},{14,22},{16,24},... | collective-permute-start | bytes 393224 | tf_op jit(solution)/shard_map/ppermute | solution.py:38
  78.9 8.7 %collective-permute-start.20 = (bf16[128,512]{1,0:T(8,128)(2,1)S(1)}, bf16[128,512]{1,0:T(8,128)(2,1)S(1)}, u32[]{:S(2)}, u32[]{:S(2)}) collective-permute-start(bf16[128,512]{1,0:T(8,128)(2,1)S(1)} %get-tuple-element.63), channel_id=1, source_target_pairs={{0,24},{2,26},{4,28},{6,30},{8,0},{10,2},{12,4},{14,6},{16,8},{18,... | collective-permute-start | bytes 393224 | tf_op jit(solution)/shard_map/ppermute | solution.py:38
  86.0 2.5 %copy-start.7 = (bf16[512,512]{1,0:T(8,128)(2,1)S(1)}, bf16[512,512]{1,0:T(8,128)(2,1)}, u32[]{:S(2)}) copy-start(bf16[512,512]{1,0:T(8,128)(2,1)} %first_ref.29) | copy-start | bytes 1572868
  86.0 2.5 %copy-start.13 = (bf16[4,512]{1,0:T(4,128)(2,1)S(1)}, bf16[4,512]{1,0:T(4,128)(2,1)}, u32[]{:S(2)}) copy-start(bf16[4,512]{1,0:T(4,128)(2,1)} %second_ref.13) | copy-start | bytes 12292
